TPU v7x, 128 devices: a whole 4x4x4 slice. The times are simulated.
128 devices in a mesh: row: 16 (over z_lo, x, core), col: 8 (over y, z_hi).
Axes of the slice: x: 4, y: 4, z: 4 (z_hi: 2, z_lo: 2; z = z_hi * 2 + z_lo), core: 2. Of those that a mesh axis runs over, the one named last changes fastest.
Arguments:
- tokens: bfloat16 [12288, 4096], P('row', 'col'), may hold values from -6 to 6
- norm_gain: bfloat16 [4096], P('col'), may hold values from 0.099609375 to 1.8984375
- qkv_weight: bfloat16 [4096, 6144], P('row', 'col'), may hold values from -1 to 1
- q_gain: float32 [128], replicated, may hold values from 2 to 8
- k_gain: float32 [128], replicated, may hold values from 1 to 3
- out_weight: bfloat16 [4096, 4096], P('row', 'col'), may hold values from -0.09375 to 0.09375
Outputs:
- attn_out: bfloat16 [12288, 4096], P('row', 'col')
All inputs are finite; a program needn't handle non-finite values.
Results may differ from a plain program's by a relative error of at most 0.013.
The roundings to bfloat16 on the way count: a program that leaves them out, or rounds other values in their place, can miss the bound.
Values may be sent and summed in bfloat16 or wider, within the bound.
A program may use at most 128 MiB of HBM per device.

v0:
```python
import math

import jax
import jax.numpy as jnp
from jax import lax
from jax.sharding import PartitionSpec as P

D = 4096
GROUP = 4


EPSILON = 1e-06
ROPE_BASE = 1000000.0


def rms_scale(values, gain):
    mean_sq = jnp.mean(values * values, axis=-1, keepdims=True)
    return values * lax.rsqrt(mean_sq + EPSILON) * gain


def rotate(values, positions):
    half = values.shape[-1] // 2
    freqs = jnp.power(
        jnp.float32(ROPE_BASE), -jnp.arange(half, dtype=jnp.float32) * 2.0 / values.shape[-1]
    )
    angles = positions.astype(jnp.float32)[:, None] * freqs[None, :]
    shape_b = (values.shape[0],) + (1,) * (values.ndim - 2) + (half,)
    cosine = jnp.cos(angles).reshape(shape_b)
    sine = jnp.sin(angles).reshape(shape_b)
    first = values[..., :half]
    second = values[..., half:]
    return jnp.concatenate(
        [first * cosine - second * sine, second * cosine + first * sine], axis=-1
    )


def per_device(tokens, norm_gain, qkv_weight, q_gain, k_gain, out_weight):
    rows = tokens.shape[0]
    head_dim = q_gain.shape[0]
    width = qkv_weight.shape[1]
    groups_here = width // ((GROUP + 2) * head_dim)
    qkv_full = lax.all_gather(qkv_weight, "row", axis=0, tiled=True)
    widened = tokens.astype(jnp.float32)
    squares_sum = lax.psum(jnp.sum(widened * widened, axis=1), "col")
    inverse = lax.rsqrt(squares_sum / D + EPSILON)
    normed = (widened * inverse[:, None] * norm_gain.astype(jnp.float32)).astype(jnp.bfloat16)
    weight_part = qkv_full
    projected = jnp.dot(
        lax.all_gather(normed, "col", axis=1, tiled=True),
        weight_part,
        preferred_element_type=jnp.float32,
    )
    blocks = projected.reshape(rows, groups_here, GROUP + 2, head_dim)
    offset = lax.axis_index("row") * rows
    positions = offset + jnp.arange(rows, dtype=jnp.int32)
    queries = rotate(rms_scale(blocks[:, :, :GROUP], q_gain), positions).astype(jnp.bfloat16)
    keys_local = rotate(rms_scale(blocks[:, :, GROUP], k_gain), positions).astype(jnp.bfloat16)
    values_local = blocks[:, :, GROUP + 1].astype(jnp.bfloat16)
    score_scale = head_dim ** (-0.5)

    def update(state, key_block, value_block, key_pos):
        running_max, running_sum, accum = state
        scores = (
            jnp.einsum("qghd,kgd->ghqk", queries, key_block, preferred_element_type=jnp.float32)
            * score_scale
        )
        allowed = key_pos[None, :] <= positions[:, None]
        masked = jnp.where(allowed, scores, -1e30)
        new_max = jnp.maximum(running_max, jnp.max(masked, axis=-1))
        weights = jnp.where(allowed, jnp.exp(masked - new_max[..., None]), 0.0)
        factor = jnp.exp(running_max - new_max)
        new_sum = running_sum * factor + jnp.sum(weights, axis=-1)
        added = jnp.einsum(
            "ghqk,kgd->ghqd",
            weights.astype(jnp.bfloat16),
            value_block,
            preferred_element_type=jnp.float32,
        )
        return (new_max, new_sum, accum * factor[..., None] + added)

    initial = (
        jnp.full((groups_here, GROUP, rows), -1e30, jnp.float32),
        jnp.zeros((groups_here, GROUP, rows), jnp.float32),
        jnp.zeros((groups_here, GROUP, rows, head_dim), jnp.float32),
    )
    keys_piece = lax.all_gather(keys_local, "row", axis=0, tiled=True)
    values_piece = lax.all_gather(values_local, "row", axis=0, tiled=True)
    count = keys_piece.shape[0]
    step_len = math.gcd(count, 512)
    num_blocks = count // step_len
    keys_blocks = keys_piece.reshape(num_blocks, step_len, groups_here, head_dim)
    values_blocks = values_piece.reshape(num_blocks, step_len, groups_here, head_dim)

    def one_block(state, inputs):
        index, key_block, value_block = inputs
        key_pos = index * step_len + jnp.arange(step_len, dtype=jnp.int32)
        return (update(state, key_block, value_block, key_pos), None)

    running_max, running_sum, accum = lax.scan(
        one_block, initial, (jnp.arange(num_blocks, dtype=jnp.int32), keys_blocks, values_blocks)
    )[0]
    attended = (
        (accum / running_sum[..., None])
        .transpose(2, 0, 1, 3)
        .reshape(rows, groups_here * GROUP * head_dim)
    )
    attended = attended.astype(jnp.bfloat16)
    out_full = lax.all_gather(out_weight, "row", axis=0, tiled=True)
    weight_part = out_full
    result = jnp.dot(
        lax.all_gather(attended, "col", axis=1, tiled=True),
        weight_part,
        preferred_element_type=jnp.float32,
    )
    return result.astype(jnp.bfloat16)


def solution(mesh):
    placed = (P("row", "col"), P("col"), P("row", "col"), P(), P(), P("row", "col"))
    return jax.shard_map(
        per_device, mesh=mesh, in_specs=placed, out_specs=P("row", "col"), check_vma=False
    )
```

profile of v0, /device:TPU:1, one launch (start us, length us, event | category | flops | bytes accessed | tf_op | source)
XLA Modules:
  0.0 674.9 jit_solution(9785540759845655344)
XLA Ops:
  7.9 22.4 %psum.7 = f32[768]{0:T(1024)S(1)} all-reduce(f32[768]{0:T(1024)S(1)} %fusion.23), channel_id=1, replica_groups=mesh['row'=16,'col'=8] {'col'}, use_global_device_ids=true, to_apply=%region_1.0 | all-reduce | flops 768 | bytes 6144 | tf_op jit(solution)/shard_map/psum | solution.py:44
  34.1 98.4 %all-gather.8.cloned.1.call-done = bf16[768,4096]{1,0:T(8,128)(2,1)} async-done(((bf16[768,512]{1,0:T(8,128)(2,1)}), bf16[768,4096]{1,0:T(8,128)(2,1)}) %all-gather.8.cloned.1.call-update) | async-done | bytes 6291472 | tf_op jit(solution)/shard_map/all_gather | solution.py:49
  132.5 44.0 %all-gather.10.cloned.1.call-done = bf16[4096,768]{1,0:T(8,128)(2,1)} async-done(((bf16[256,768]{1,0:T(8,128)(2,1)}), bf16[4096,768]{1,0:T(8,128)(2,1)}) %all-gather.10.cloned.1.call-update) | async-done | bytes 6291472 | tf_op jit(solution)/shard_map/all_gather | solution.py:42
  176.5 9.1 %fusion.34 = f32[768,768]{0,1:T(8,128)S(1)} fusion(bf16[768,4096]{1,0:T(8,128)(2,1)} %all-gather.8.cloned.1.call-done, bf16[4096,768]{1,0:T(8,128)(2,1)} %all-gather.10.cloned.1.call-done), kind=kOutput, calls=%fused_computation.64 | convolution fusion | flops 4831838208 | bytes 14942208 | tf_op jit(solution)/shard_map/dot_general | solution.py:48
  195.4 28.5 %all-gather.12.cloned.1.call-done = bf16[12288,1,128]{0,2,1:T(8,128)(2,1)} async-done(((bf16[768,1,128]{0,2,1:T(8,128)(2,1)}), bf16[12288,1,128]{0,2,1:T(8,128)(2,1)}) %all-gather.12.cloned.1.call-update) | async-done | bytes 3145744 | tf_op jit(solution)/shard_map/all_gather | solution.py:86
  223.9 4.7 copy.12
  228.5 32.9 %all-gather.18.cloned.1.call-done = bf16[12288,1,1,128]{0,3,2,1:T(8,128)(2,1)} async-done(((bf16[768,1,1,128]{0,3,2,1:T(8,128)(2,1)}), bf16[12288,1,1,128]{0,3,2,1:T(8,128)(2,1)}) %all-gather.18.cloned.1.call-update) | async-done | bytes 3145744 | tf_op jit(solution)/shard_map/all_gather | solution.py:87
  261.4 4.6 copy.14
  266.1 302.7 %while.15 = (s32[]{:T(128)}, f32[1,4,768]{2,1,0:T(4,128)S(1)}, f32[1,4,768]{2,1,0:T(4,128)S(1)}, f32[1,4,768,128]{3,2,1,0:T(8,128)S(1)}, s32[24]{0:T(128)S(1)}, ...) while((s32[]{:T(128)}, f32[1,4,768]{2,1,0:T(4,128)S(1)}, ...), condition=%wide.region_7.8_spmd.clone, body=%wide.region_4.7_spmd.clone.sunk | while | flops 827346176 | bytes 50015416 | solution.py:99
  267.6 4.7 fusion.46
  272.4 4.4 bitcast_add_fusion.5
  280.3 4.7 fusion.46
  285.1 4.5 bitcast_add_fusion.5
  293.1 4.7 fusion.46
  297.9 4.4 bitcast_add_fusion.5
  305.7 4.7 fusion.46
  310.5 4.4 bitcast_add_fusion.5
  318.3 4.7 fusion.46
  323.1 4.4 bitcast_add_fusion.5
  330.9 4.7 fusion.46
  335.7 4.4 bitcast_add_fusion.5
  343.5 4.7 fusion.46
  348.3 4.4 bitcast_add_fusion.5
  356.1 4.7 fusion.46
  360.9 4.4 bitcast_add_fusion.5
  368.7 4.7 fusion.46
  373.5 4.4 bitcast_add_fusion.5
  381.3 4.7 fusion.46
  386.1 4.4 bitcast_add_fusion.5
  393.9 4.7 fusion.46
  406.5 4.7 fusion.46
  419.1 4.7 fusion.46
  431.7 4.7 fusion.46
  444.3 4.7 fusion.46
  449.1 4.4 bitcast_add_fusion.5
  456.9 4.7 fusion.46
  469.5 4.7 fusion.46
  482.1 4.7 fusion.46
  494.7 4.7 fusion.46
  499.5 4.4 bitcast_add_fusion.5
  507.3 4.7 fusion.46
  519.9 4.7 fusion.46
  532.5 4.7 fusion.46
  545.1 4.7 fusion.46
  549.9 4.4 bitcast_add_fusion.5
  557.7 4.7 fusion.46
  570.3 89.4 %all-gather.14.cloned.1.call-done = bf16[768,4096]{0,1:T(8,128)(2,1)} async-done(((bf16[768,512]{0,1:T(8,128)(2,1)}), bf16[768,4096]{0,1:T(8,128)(2,1)}) %all-gather.14.cloned.1.call-update) | async-done | bytes 6291472 | tf_op jit(solution)/shard_map/all_gather | solution.py:111
  659.7 8.3 %convolution_convert_fusion = bf16[768,512]{1,0:T(8,128)(2,1)} fusion(bf16[768,4096]{0,1:T(8,128)(2,1)} %all-gather.14.cloned.1.call-done, bf16[4096,512]{1,0:T(8,128)(2,1)} %all-gather.16.cloned.1.call-done), kind=kOutput, calls=%fused_computation.40 | convolution fusion | flops 3221618688 | bytes 11272192 | tf_op jit(solution)/shard_map/dot_general | solution.py:110
  (302 shorter events, 131.3 us)
Async XLA Ops:
  6.5 125.9 %all-gather.8.cloned.1.call-start = ((), (), s32[]{:S(2)}) async-start(), calls=%async_computation | async-start | bytes 7077888 | tf_op jit(solution)/shard_map/all_gather | solution.py:49
  33.2 143.2 %all-gather.10.cloned.1.call-start = ((), (), s32[]{:S(2)}) async-start(), calls=%async_computation.1 | async-start | bytes 6684672 | tf_op jit(solution)/shard_map/all_gather | solution.py:42
  34.0 189.9 %all-gather.12.cloned.1.call-start = ((), (), s32[]{:S(2)}) async-start(), calls=%async_computation.2 | async-start | bytes 3342336 | tf_op jit(solution)/shard_map/all_gather | solution.py:86
  34.1 151.6 %copy-start.5 = (f32[128]{0:T(128)S(1)}, f32[128]{0:T(128)}, u32[]{:S(2)}) copy-start(f32[128]{0:T(128)} %param.12) | copy-start | bytes 1540
  185.6 5.7 copy-start.1
  187.3 74.1 %all-gather.18.cloned.1.call-start = ((), (), s32[]{:S(2)}) async-start(), calls=%async_computation.5 | async-start | bytes 3342336 | tf_op jit(solution)/shard_map/all_gather | solution.py:87
  188.0 382.2 %all-gather.16.cloned.1.call-start = ((), (), s32[]{:S(2)}) async-start(), calls=%async_computation.4 | async-start | bytes 4456448 | tf_op jit(solution)/shard_map/all_gather | solution.py:108
  188.6 471.1 %all-gather.14.cloned.1.call-start = ((), (), s32[]{:S(2)}) async-start(), calls=%async_computation.3 | async-start | bytes 7077888 | tf_op jit(solution)/shard_map/all_gather | solution.py:111
  192.8 1.0 copy-start.6
  193.3 1.0 copy-start.3
  228.5 37.5 %copy-start.2 = (f32[1,4,768,128]{3,2,1,0:T(8,128)S(1)}, f32[1,4,768,128]{3,2,1,0:T(8,128)}, u32[]{:S(2)}) copy-start(f32[1,4,768,128]{3,2,1,0:T(8,128)} %custom-call.2) | copy-start | bytes 4718596
  228.5 37.5 %copy-start.4 = (f32[1,4,768]{2,1,0:T(4,128)S(1)}, f32[1,4,768]{2,1,0:T(4,128)}, u32[]{:S(2)}) copy-start(f32[1,4,768]{2,1,0:T(4,128)} %custom-call.1) | copy-start | bytes 36868
  272.4 4.8 copy-start
  285.1 4.9 copy-start
  297.9 4.7 copy-start
  310.5 4.7 copy-start
  323.1 4.7 copy-start
  335.7 4.7 copy-start
  348.3 4.7 copy-start
  360.9 4.7 copy-start
  373.5 4.7 copy-start
  386.1 4.7 copy-start
  398.7 4.7 copy-start
  411.3 4.7 copy-start
  423.9 4.7 copy-start
  436.5 4.7 copy-start
  449.1 4.7 copy-start
  461.7 4.7 copy-start
  474.3 4.7 copy-start
  486.9 4.7 copy-start
  499.5 4.7 copy-start
  512.0 4.7 copy-start
  524.6 4.7 copy-start
  537.2 4.7 copy-start
  549.8 4.7 copy-start
  562.4 4.7 copy-start
Sparse Core Ops, SparseCore 0:
  33.4 99.0 all-gather.7
  134.2 42.2 all-gather.9
  187.4 36.4 all-gather.11
  225.4 35.9 all-gather.17
  263.0 37.6 all-gather.15
  570.4 89.2 all-gather.13
where the time goes:
time: 676 us; the launch traced here: 675 us
  waiting for transfers between devices  294 us (43%)
  matrix products  236 us (35%)
  other arithmetic  57.1 us (8%)
  local copies, waits for them, and re-layouts  33.7 us (5%)
  blocking collectives  22.4 us (3%)
  loops' own time  17.3 us (3%)
  between operations  13.7 us (2%)
    dot_general x24, matrix products, update(): jnp.einsum('qghd,kgd->ghqk', queries, key_block, preferred_element_type=j...  113 us
    dot_general x24, matrix products, update(): jnp.einsum('ghqk,kgd->ghqd', weights.astype(jnp.bfloat16), value_block, p...  105 us
    all_gather x1, waiting for transfers between devices, per_device(): lax.all_gather(normed, 'col', axis=1, tiled=True)  98.4 us
    all_gather x1, waiting for transfers between devices, per_device(): lax.all_gather(attended, 'col', axis=1, tiled=True)  89.4 us
    all_gather x1, waiting for transfers between devices, per_device(): qkv_full = lax.all_gather(qkv_weight, 'row', axis=0, tiled=True)  44 us
    reduce_sum x24, other arithmetic, update(): new_sum = running_sum * factor + jnp.sum(weights, axis=-1)  37.7 us
    all_gather x1, waiting for transfers between devices, per_device(): values_piece = lax.all_gather(values_local, 'row', axis=0, tiled=True)  32.9 us
    all_gather x1, waiting for transfers between devices, per_device(): keys_piece = lax.all_gather(keys_local, 'row', axis=0, tiled=True)  28.5 us
  transfers between devices with their start and end apart: 6, of which 5 were waited for; matrix products, arithmetic and copies ran while one was open for 44% of the time, Pallas kernels for 0%

commit v1 on v0

v1 whole, which is shorter than its diff:
```python
import functools
import math

import jax
import jax.numpy as jnp
from jax import lax
from jax.experimental import pallas as pl
from jax.experimental.pallas import tpu as pltpu
from jax.sharding import PartitionSpec as P

D = 4096
GROUP = 4
EPSILON = 1e-06
ROPE_BASE = 1000000.0
KEY_BLOCK = 768


def rms_scale(values, gain):
    mean_sq = jnp.mean(values * values, axis=-1, keepdims=True)
    return values * lax.rsqrt(mean_sq + EPSILON) * gain


def rotate(values, cosine, sine):
    half = values.shape[-1] // 2
    first = values[..., :half]
    second = values[..., half:]
    return jnp.concatenate(
        [first * cosine - second * sine, second * cosine + first * sine], axis=-1
    )


def flash_kernel(devices, scale, q_ref, kv_ref, o_ref, acc, top):
    rows = q_ref.shape[0]
    head_dim = kv_ref.shape[1] // 2
    chunk = pl.program_id(0)
    me = lax.axis_index("row")
    index = jnp.where(chunk == 0, 2 * me, 2 * devices - 1 - 2 * me)
    acc[...] = jnp.zeros_like(acc)
    top[...] = jnp.full_like(top, -1e30)
    factor_log2 = scale * math.log2(math.e)
    ones = jnp.ones((KEY_BLOCK, head_dim), jnp.bfloat16)

    def scores(h, keys):
        return lax.dot_general(
            q_ref[:, h * head_dim : (h + 1) * head_dim],
            keys,
            (((1,), (1,)), ((), ())),
            preferred_element_type=jnp.float32,
        )

    def step(block, allowed):
        start = pl.multiple_of(block * KEY_BLOCK, KEY_BLOCK)
        keys = kv_ref[pl.ds(start, KEY_BLOCK), :head_dim]
        values = kv_ref[pl.ds(start, KEY_BLOCK), head_dim:]
        wide = jnp.concatenate([values, ones], axis=1)
        following = scores(0, keys)
        for h in range(GROUP):
            raw = following
            if h + 1 < GROUP:
                following = scores(h + 1, keys)
            if allowed is not None:
                raw = jnp.where(allowed, raw, -1e30)
            before = top[h]
            now = jnp.maximum(before, jnp.max(raw, axis=-1, keepdims=True))
            shift = now[:, :1] * factor_log2
            weights = jnp.exp2(raw * factor_log2 - shift).astype(jnp.bfloat16)
            fade = jnp.exp2((before - now) * factor_log2)
            added = jnp.dot(weights, wide, preferred_element_type=jnp.float32)
            acc[h] = acc[h] * jnp.concatenate([fade, fade], axis=1) + added
            top[h] = now

    full = index // 2

    @pl.loop(0, full)
    def _(block):
        step(block, None)

    key_pos = full * KEY_BLOCK + lax.broadcasted_iota(jnp.int32, (rows, KEY_BLOCK), 1)
    query_pos = index * rows + lax.broadcasted_iota(jnp.int32, (rows, KEY_BLOCK), 0)
    step(full, key_pos <= query_pos)
    for h in range(GROUP):
        o_ref[:, h * head_dim : (h + 1) * head_dim] = (
            acc[h, :, :head_dim] / acc[h, :, head_dim:]
        ).astype(o_ref.dtype)


def flash(devices, scale, queries, keys_values):
    rows, width = queries.shape
    half = rows // 2
    head_dim = width // GROUP
    return pl.pallas_call(
        functools.partial(flash_kernel, devices, scale),
        out_shape=jax.ShapeDtypeStruct(queries.shape, jnp.bfloat16),
        grid=(2,),
        in_specs=[
            pl.BlockSpec((half, width), lambda i: (i, 0)),
            pl.BlockSpec(keys_values.shape, lambda i: (0, 0), pipeline_mode=pl.Buffered(1)),
        ],
        out_specs=pl.BlockSpec((half, width), lambda i: (i, 0)),
        scratch_shapes=[
            pltpu.VMEM((GROUP, half, 2 * head_dim), jnp.float32),
            pltpu.VMEM((GROUP, half, head_dim), jnp.float32),
        ],
        compiler_params=pltpu.CompilerParams(vmem_limit_bytes=48 * 1024 * 1024),
        cost_estimate=pl.CostEstimate(
            flops=10_000_000_000, bytes_accessed=8_000_000, transcendentals=20_000_000
        ),
    )(queries, keys_values)


def per_device(devices, tokens, norm_gain, qkv_weight, q_gain, k_gain, out_weight):
    rows = tokens.shape[0]
    half = rows // 2
    head_dim = q_gain.shape[0]
    tokens_full = lax.all_gather(tokens, "col", axis=1, tiled=True)
    gain_full = lax.all_gather(norm_gain, "col", axis=0, tiled=True)
    qkv_full = lax.all_gather(qkv_weight, "row", axis=0, tiled=True)
    widened = tokens_full.astype(jnp.float32)
    mean_sq = jnp.mean(widened * widened, axis=1, keepdims=True)
    normed = (widened * lax.rsqrt(mean_sq + EPSILON) * gain_full.astype(jnp.float32)).astype(
        jnp.bfloat16
    )
    projected = jnp.dot(normed, qkv_full, preferred_element_type=jnp.float32)
    me = lax.axis_index("row")
    positions = me * rows + jnp.arange(rows, dtype=jnp.int32)
    freqs = jnp.power(
        jnp.float32(ROPE_BASE),
        -jnp.arange(head_dim // 2, dtype=jnp.float32) * 2.0 / head_dim,
    )
    angles = positions.astype(jnp.float32)[:, None] * freqs[None, :]
    cosine, sine = jnp.cos(angles), jnp.sin(angles)
    pieces = [projected[:, i * head_dim : (i + 1) * head_dim] for i in range(GROUP + 2)]
    queries = jnp.concatenate(
        [rotate(rms_scale(u, q_gain), cosine, sine).astype(jnp.bfloat16) for u in pieces[:GROUP]],
        axis=1,
    )
    keys = rotate(rms_scale(pieces[GROUP], k_gain), cosine, sine).astype(jnp.bfloat16)
    values = pieces[GROUP + 1].astype(jnp.bfloat16)
    swap = [(i, devices - 1 - i) for i in range(devices)]
    keys_values = lax.all_gather(
        jnp.concatenate([keys, values], axis=1), "row", axis=0, tiled=True
    )
    balanced = jnp.concatenate(
        [queries[:half], lax.ppermute(queries[half:], "row", swap)], axis=0
    )
    attended = flash(devices, head_dim ** (-0.5), balanced, keys_values)
    attended = jnp.concatenate(
        [attended[:half], lax.ppermute(attended[half:], "row", swap)], axis=0
    )
    out_full = lax.all_gather(out_weight, "row", axis=0, tiled=True)
    result = jnp.dot(
        lax.all_gather(attended, "col", axis=1, tiled=True),
        out_full,
        preferred_element_type=jnp.float32,
    )
    return result.astype(jnp.bfloat16)


def solution(mesh):
    placed = (P("row", "col"), P("col"), P("row", "col"), P(), P(), P("row", "col"))
    return jax.shard_map(
        functools.partial(per_device, mesh.shape["row"]),
        mesh=mesh,
        in_specs=placed,
        out_specs=P("row", "col"),
        check_vma=False,
    )
```

time: 676 us -> 382 us (0.57)
  matrix products: 236 us -> 17.5 us
  other arithmetic: 57.1 us -> 11.2 us
  Pallas kernels: 0 us -> 37.1 us
  local copies, waits for them, and re-layouts: 33.7 us -> 1.53 us
  waiting for transfers between devices: 294 us -> 269 us
  loops' own time: 17.3 us -> 0 us
    dot_general x50 -> x2, matrix products: 236 us -> 17.5 us  [the longest x1 9.21 us: per_device(): projected = jnp.dot(normed, qkv_full, preferred_element_type=jnp.float32)]
    all_gather x3 -> x2, waiting for transfers between devices: 160 us -> 107 us  [the longest x1 75.4 us: per_device(): tokens_full = lax.all_gather(tokens, 'col', axis=1, tiled=True)]
    pallas_call x0 -> x1, Pallas kernels: none -> 37.1 us  [flash(): pl.pallas_call(functools.partial(flash_kernel, devices, scale), out_shape...]
    reduce_sum x25 -> x1, other arithmetic: 39.1 us -> 4.07 us  [per_device(): mean_sq = jnp.mean(widened * widened, axis=1, keepdims=True)]
    all_gather x0 -> x1, blocking collectives: none -> 27.2 us  [per_device(): gain_full = lax.all_gather(norm_gain, 'col', axis=0, tiled=True)]
    psum x1 -> x0, blocking collectives: 22.4 us -> none  [per_device(): squares_sum = lax.psum(jnp.sum(widened * widened, axis=1), 'col')]
    ppermute x0 -> x2, waiting for transfers between devices: none -> 20.8 us  [the longest x1 10.5 us: per_device(): lax.ppermute(queries[half:], 'row', swap)]
    another operation x1 -> x0, loops' own time: 17.3 us -> none  [per_device(): lax.scan(one_block, initial, (jnp.arange(num_blocks, dtype=jnp.int32), ke...]
  transfers between devices with their start and end apart: 6 -> 7, of which waited for: 5 -> 6; matrix products, arithmetic and copies ran while one was open for 44% -> 2% of each run, Pallas kernels for 0% -> 10%
where the time goes in v1:
time: 382 us
  waiting for transfers between devices  269 us (70%)
  Pallas kernels  37.1 us (10%)
  blocking collectives  27.2 us (7%)
  matrix products  17.5 us (5%)
  between operations  13.3 us (3%)
  other arithmetic  11.2 us (3%)
  starting transfers between devices  5.76 us (2%)
    all_gather x1, waiting for transfers between devices, per_device(): lax.all_gather(attended, 'col', axis=1, tiled=True)  98.9 us
    all_gather x1, waiting for transfers between devices, per_device(): tokens_full = lax.all_gather(tokens, 'col', axis=1, tiled=True)  75.4 us
    all_gather x1, waiting for transfers between devices, per_device(): qkv_full = lax.all_gather(qkv_weight, 'row', axis=0, tiled=True)  39.9 us
    pallas_call x1, Pallas kernels, flash(): pl.pallas_call(functools.partial(flash_kernel, devices, scale), out_shape...  37.1 us
    all_gather x1, waiting for transfers between devices, per_device(): lax.all_gather(jnp.concatenate([keys, values], axis=1), 'row', axis=0, ti...  31.4 us
    all_gather x1, blocking collectives, per_device(): gain_full = lax.all_gather(norm_gain, 'col', axis=0, tiled=True)  27.2 us
    ppermute x1, waiting for transfers between devices, per_device(): lax.ppermute(queries[half:], 'row', swap)  10.5 us
    ppermute x1, waiting for transfers between devices, per_device(): lax.ppermute(attended[half:], 'row', swap)  10.4 us
  transfers between devices with their start and end apart: 7, of which 6 were waited for; matrix products, arithmetic and copies ran while one was open for 2% of the time, Pallas kernels for 10%

profile of v1, /device:TPU:1, one launch (start us, length us, event | category | flops | bytes accessed | tf_op | source)
XLA Modules:
  0.0 382.1 jit_solution(1272926683582761061)
XLA Ops:
  6.5 0.0 all-gather.7.cloned.1.call-start
  6.5 0.7 all-gather.7.cloned.1.call-update
  7.3 0.0 all-gather.9.cloned.1.call-start
  7.3 0.7 all-gather.9.cloned.1.call-update
  8.0 0.0 all-gather.11.cloned.1.call-start
  8.1 0.7 reshape.62
  8.7 27.2 %all-gather = bf16[8,1,512]{2,1,0:T(2,128)(2,1)S(1)} all-gather(bf16[1,1,512]{2,1,0:T(2,128)(2,1)S(1)} %reshape.62), channel_id=1, replica_groups=mesh['row'=16,'col'=8] {'col'}, dimensions={0}, use_global_device_ids=true | all-gather | bytes 9216 | tf_op jit(solution)/shard_map/all_gather | solution.py:116
  36.0 75.4 %all-gather.7.cloned.1.call-done = bf16[768,4096]{1,0:T(8,128)(2,1)} async-done(((bf16[768,512]{1,0:T(8,128)(2,1)}), bf16[768,4096]{1,0:T(8,128)(2,1)}) %all-gather.7.cloned.1.call-update) | async-done | bytes 6291472 | tf_op jit(solution)/shard_map/all_gather | solution.py:115
  111.5 4.1 %fusion = f32[768]{0:T(1024)S(1)} fusion(bf16[768,4096]{1,0:T(8,128)(2,1)} %all-gather.7.cloned.1.call-done), kind=kLoop, calls=%fused_computation.2 | loop fusion | flops 9436416 | bytes 6294528 | tf_op jit(solution)/shard_map/reduce_sum | solution.py:119
  115.5 39.9 %all-gather.9.cloned.1.call-done = bf16[4096,768]{1,0:T(8,128)(2,1)} async-done(((bf16[256,768]{1,0:T(8,128)(2,1)}), bf16[4096,768]{1,0:T(8,128)(2,1)}) %all-gather.9.cloned.1.call-update) | async-done | bytes 6291472 | tf_op jit(solution)/shard_map/all_gather | solution.py:117
  155.5 0.0 copy-start
  155.5 0.0 copy-start.1
  155.5 9.2 %fusion.3 = f32[768,768]{1,0:T(8,128)S(1)} fusion(bf16[4096,768]{1,0:T(8,128)(2,1)} %all-gather.9.cloned.1.call-done, bf16[768,4096]{1,0:T(8,128)(2,1)} %all-gather.7.cloned.1.call-done, f32[4096]{0:T(1024)S(1)} %bitcast.4, f32[768]{0:T(1024)S(1)} %add_rsqrt_fusion.5), kind=kOutput, calls=%fused_computation.5 | convolution fusion | flops 4844421120 | bytes 14961664 | tf_op jit(solution)/shard_map/dot_general | solution.py:123
  164.7 0.6 multiply_reduce_fusion
  165.4 0.0 copy-done
  165.4 0.0 copy-done.1
  165.4 0.6 multiply_multiply_fusion.1
  166.0 2.1 fusion.44
  168.1 0.9 pad_maximum_fusion.2
  169.0 0.0 all-gather.11.cloned.1.call-update
  169.1 0.0 all-gather.15.cloned.1.call-start
  169.1 0.5 all-gather.15.cloned.1.call-update
  169.6 0.0 all-gather.13.cloned.1.call-start
  169.7 1.8 fusion.30
  171.5 0.7 concatenate.24
  172.2 0.1 fusion.48
  172.3 2.8 collective-permute-start
  175.1 10.5 %collective-permute-done = bf16[384,512]{1,0:T(8,128)(2,1)S(1)} collective-permute-done((bf16[384,512]{1,0:T(8,128)(2,1)S(1)}, bf16[384,512]{1,0:T(8,128)(2,1)S(1)}, u32[]{:S(2)}, u32[]{:S(2)}) %collective-permute-start) | collective-permute-done | bytes 393248 | tf_op jit(solution)/shard_map/ppermute | solution.py:144
  185.6 0.1 pad_maximum_fusion.q_ref
  185.6 31.4 %all-gather.11.cloned.1.call-done.kv_ref = bf16[12288,256]{1,0:T(8,128)(2,1)} async-done(((bf16[768,256]{1,0:T(8,128)(2,1)}), bf16[12288,256]{1,0:T(8,128)(2,1)}) %all-gather.11.cloned.1.call-update) | async-done | bytes 6291472 | tf_op jit(solution)/shard_map/all_gather | solution.py:140
  217.1 37.1 %shard_map.64 = bf16[768,512]{1,0:T(8,128)(2,1)S(1)} custom-call(bf16[768,512]{1,0:T(8,128)(2,1)S(1)} %pad_maximum_fusion.q_ref, bf16[12288,256]{1,0:T(8,128)(2,1)} %all-gather.11.cloned.1.call-done.kv_ref), custom_call_target="tpu_custom_call" | custom-call | flops 10000000000 | bytes 8000000 | tf_op jit(solution)/shard_map/pallas_call | solution.py:91
  254.2 0.1 fusion.47
  254.3 2.8 collective-permute-start.1
  257.1 10.4 %collective-permute-done.1 = bf16[384,512]{1,0:T(8,128)(2,1)S(1)} collective-permute-done((bf16[384,512]{1,0:T(8,128)(2,1)S(1)}, bf16[384,512]{1,0:T(8,128)(2,1)S(1)}, u32[]{:S(2)}, u32[]{:S(2)}) %collective-permute-start.1) | collective-permute-done | bytes 393248 | tf_op jit(solution)/shard_map/ppermute | solution.py:148
  267.4 0.9 pad_maximum_fusion.1
  268.4 0.0 all-gather.13.cloned.1.call-update
  268.4 0.0 all-gather.15.cloned.1.call-done
  268.4 98.9 %all-gather.13.cloned.1.call-done = bf16[768,4096]{1,0:T(8,128)(2,1)} async-done(((bf16[768,512]{1,0:T(8,128)(2,1)}), bf16[768,4096]{1,0:T(8,128)(2,1)}) %all-gather.13.cloned.1.call-update) | async-done | bytes 6291472 | tf_op jit(solution)/shard_map/all_gather | solution.py:152
  367.3 8.3 %convolution_convert_fusion = bf16[768,512]{1,0:T(8,128)(2,1)} fusion(bf16[768,4096]{1,0:T(8,128)(2,1)} %all-gather.13.cloned.1.call-done, bf16[4096,512]{1,0:T(8,128)(2,1)} %all-gather.15.cloned.1.call-done), kind=kOutput, calls=%fused_computation.8 | convolution fusion | flops 3221618688 | bytes 11272192 | tf_op jit(solution)/shard_map/dot_general | solution.py:151
  (8 shorter events, 0.1 us)
Async XLA Ops:
  6.5 104.9 %all-gather.7.cloned.1.call-start = ((), (), s32[]{:S(2)}) async-start(), calls=%async_computation | async-start | bytes 7077888 | tf_op jit(solution)/shard_map/all_gather | solution.py:115
  7.3 148.2 %all-gather.9.cloned.1.call-start = ((), (), s32[]{:S(2)}) async-start(), calls=%async_computation.1 | async-start | bytes 6684672 | tf_op jit(solution)/shard_map/all_gather | solution.py:117
  8.0 209.1 %all-gather.11.cloned.1.call-start = ((), (), s32[]{:S(2)}) async-start(), calls=%async_computation.2 | async-start | bytes 6684672 | tf_op jit(solution)/shard_map/all_gather | solution.py:140
  155.5 9.9 %copy-start = (f32[128]{0:T(128)S(1)}, f32[128]{0:T(128)}, u32[]{:S(2)}) copy-start(f32[128]{0:T(128)} %param.9) | copy-start | bytes 1540
  155.5 9.9 %copy-start.1 = (f32[128]{0:T(128)S(1)}, f32[128]{0:T(128)}, u32[]{:S(2)}) copy-start(f32[128]{0:T(128)} %param.10) | copy-start | bytes 1540
  169.1 99.3 %all-gather.15.cloned.1.call-start = ((), (), s32[]{:S(2)}) async-start(), calls=%async_computation.4 | async-start | bytes 4456448 | tf_op jit(solution)/shard_map/all_gather | solution.py:150
  169.6 197.7 %all-gather.13.cloned.1.call-start = ((), (), s32[]{:S(2)}) async-start(), calls=%async_computation.3 | async-start | bytes 7077888 | tf_op jit(solution)/shard_map/all_gather | solution.py:152
  172.3 13.3 %collective-permute-start = (bf16[384,512]{1,0:T(8,128)(2,1)S(1)}, bf16[384,512]{1,0:T(8,128)(2,1)S(1)}, u32[]{:S(2)}, u32[]{:S(2)}) collective-permute-start(bf16[384,512]{1,0:T(8,128)(2,1)S(1)} %get-tuple-element.18), channel_id=1, source_target_pairs={{0,120},{8,112},{16,104},{24,96},{32,88},{40,80},{48,72},{56,64},{... | collective-permute-start | bytes 1179656 | tf_op jit(solution)/shard_map/ppermute | solution.py:144
  254.3 13.2 %collective-permute-start.1 = (bf16[384,512]{1,0:T(8,128)(2,1)S(1)}, bf16[384,512]{1,0:T(8,128)(2,1)S(1)}, u32[]{:S(2)}, u32[]{:S(2)}) collective-permute-start(bf16[384,512]{1,0:T(8,128)(2,1)S(1)} %get-tuple-element.16), channel_id=1, source_target_pairs={{0,120},{8,112},{16,104},{24,96},{32,88},{40,80},{48,72},{56,64},{... | collective-permute-start | bytes 1179656 | tf_op jit(solution)/shard_map/ppermute | solution.py:148
Sparse Core Ops, SparseCore 0:
  9.5 101.8 all-gather.6
  113.2 42.2 all-gather.8
  169.2 47.8 all-gather.10
  218.6 37.9 all-gather.14
  268.5 98.7 all-gather.12

commit v2 on v1

--- a/solution.py
+++ b/solution.py
@@ -13,28 +13,399 @@
 EPSILON = 1e-06
 ROPE_BASE = 1000000.0
 KEY_BLOCK = 768
-
-
-def rms_scale(values, gain):
-    mean_sq = jnp.mean(values * values, axis=-1, keepdims=True)
-    return values * lax.rsqrt(mean_sq + EPSILON) * gain
-
-
-def rotate(values, cosine, sine):
-    half = values.shape[-1] // 2
-    first = values[..., :half]
-    second = values[..., half:]
-    return jnp.concatenate(
-        [first * cosine - second * sine, second * cosine + first * sine], axis=-1
-    )
-
-
-def flash_kernel(devices, scale, q_ref, kv_ref, o_ref, acc, top):
+MESH = pl.DeviceIdType.MESH
+
+
+def ring(value, shift):
+    return (value + shift + 4) % 4
+
+
+class Place:
+    def __init__(self):
+        row, col = lax.axis_index("row"), lax.axis_index("col")
+        self.z_lo, self.x, self.core = row // 8, (row // 2) % 4, row % 2
+        self.y, self.z_hi = col // 2, col % 2
+        self.z = 2 * self.z_hi + self.z_lo
+
+    def device(self, **at):
+        z = at.get("z", self.z)
+        z_lo, z_hi = at.get("z_lo", z % 2), at.get("z_hi", z // 2)
+        x, y, core = at.get("x", self.x), at.get("y", self.y), at.get("core", self.core)
+        return {"row": 8 * z_lo + 2 * x + core, "col": 2 * y + z_hi}
+
+    def step(self, axis, shift):
+        return self.device(**{axis: ring(getattr(self, axis), shift)})
+
+    def other_core(self):
+        return self.device(core=1 - self.core)
+
+    def turned(self):
+        return self.device(core=self.z_hi, z_hi=self.core, z_lo=self.z_lo)
+
+    def mirrored(self, bit):
+        return self.z_lo + bit - 2 * bit * self.z_lo, self.x + bit * (3 - 2 * self.x)
+
+    def chunk_to(self, half):
+        z_lo, x = self.mirrored(self.core)
+        return self.device(z_lo=z_lo, x=x, core=self.z_hi, z_hi=(self.core + half) % 2)
+
+    def chunk_from(self, half):
+        core = (self.z_hi + half) % 2
+        z_lo, x = self.mirrored(core)
+        return self.device(z_lo=z_lo, x=x, core=core, z_hi=self.core)
+
+    def column(self, y=None, core=None):
+        y = self.y if y is None else y
+        return 2 * y + (self.core if core is None else core)
+
+    def location(self, x, z):
+        return 8 * (z % 2) + 2 * x + z // 2
+
+    def chunk(self, half, x, z):
+        first = 16 * (z % 2) + 4 * x + z // 2
+        return first if half == 0 else 31 - first
+
+
+class Net:
+    def __init__(self, sent, landed, base=0):
+        self.sent, self.landed, self.base, self.copies = sent, landed, base, []
+
+    def send(self, ref, to, target=None):
+        i = self.base + len(self.copies)
+        copy = pltpu.make_async_remote_copy(
+            src_ref=ref,
+            dst_ref=ref if target is None else target,
+            send_sem=self.sent.at[i],
+            recv_sem=self.landed.at[i],
+            device_id=to,
+            device_id_type=MESH,
+        )
+        copy.start()
+        self.copies.append(copy)
+        return copy
+
+    def finish(self):
+        for copy in self.copies:
+            copy.wait_send()
+
+
+def greet(partners):
+    barrier = pltpu.get_barrier_semaphore()
+    for partner in partners:
+        pl.semaphore_signal(barrier, inc=1, device_id=partner, device_id_type=MESH)
+    pl.semaphore_wait(barrier, len(partners))
+
+
+def plane_gather(net, here, full, rows, spot, own=None):
+    axes = (("x", "z"), ("z", "x"))
+    piece = rows // 2
+
+    def at(half, first, second):
+        x = ring(here.x, first if half == 0 else second)
+        z = ring(here.z, second if half == 0 else first)
+        return pl.multiple_of(spot(half, x, z), rows)
+
+    def block(half, first, second):
+        return full.at[pl.ds(at(half, first, second), rows), :]
+
+    def part(half, first, second, way):
+        start = at(half, first, second) + (0 if way == 1 else piece)
+        return full.at[pl.ds(pl.multiple_of(start, piece), piece), :]
+
+    def mine(half):
+        return block(half, 0, 0) if own is None else own(half)
+
+    one, two, onward, last = {}, {}, {}, {}
+    both = [(half, way) for half in (0, 1) for way in (1, -1)]
+    for half, way in both:
+        one[half, way] = net.send(
+            mine(half), here.step(axes[half][0], way), block(half, 0, 0)
+        )
+    for half, way in both:
+        two[half, 0, way] = net.send(
+            mine(half), here.step(axes[half][1], way), block(half, 0, 0)
+        )
+    yield
+    for half, way in both:
+        one[half, way].wait_recv()
+        onward[half, way] = net.send(
+            part(half, -way, 0, way), here.step(axes[half][0], way)
+        )
+    for half, way in both:
+        for turn in (1, -1):
+            two[half, -way, turn] = net.send(
+                block(half, -way, 0), here.step(axes[half][1], turn)
+            )
+    yield
+    for half, way in both:
+        two[half, 0, way].wait_recv()
+        last[half, 0, way] = net.send(
+            part(half, 0, -way, way), here.step(axes[half][1], way)
+        )
+    yield
+    for half, way in both:
+        onward[half, way].wait_recv()
+    for half, way in both:
+        two[half, 2, way] = net.send(block(half, 2, 0), here.step(axes[half][1], way))
+    yield
+    for where in (-1, 1, 2):
+        for half, way in both:
+            two[half, where, way].wait_recv()
+            last[half, where, way] = net.send(
+                part(half, where, -way, way), here.step(axes[half][1], way)
+            )
+        yield
+    for copy in last.values():
+        copy.wait_recv()
+
+
+def column_gather(net, here, full, width, own=None):
+    rows = full.shape[0]
+    piece = rows // 2
+
+    def part(y, which):
+        start = pl.multiple_of(here.column(y) * width, width)
+        rows_of = slice(which * piece, (which + 1) * piece) if which < 2 else slice(None)
+        return full.at[rows_of, pl.ds(start, width)]
+
+    def mine(which):
+        if own is None:
+            return part(here.y, which)
+        return own.at[slice(which * piece, (which + 1) * piece) if which < 2 else slice(None), :]
+
+    far = {1: 0, -1: 1}
+    near, onward, across = {}, {}, []
+    for late in (0, 1):
+        for way in (1, -1):
+            which = far[way] if late == 0 else 1 - far[way]
+            near[way, late] = net.send(mine(which), here.step("y", way), part(here.y, which))
+    across.append(net.send(mine(2), here.other_core(), part(here.y, 2)))
+    yield
+    for way in (1, -1):
+        near[way, 0].wait_recv()
+        onward[way] = net.send(part(ring(here.y, -way), far[way]), here.step("y", way))
+    yield
+    for way in (1, -1):
+        near[way, 1].wait_recv()
+        across.append(net.send(part(ring(here.y, -way), 2), here.other_core()))
+    yield
+    yield
+    for way in (1, -1):
+        onward[way].wait_recv()
+        across.append(net.send(part(ring(here.y, 2), far[way]), here.other_core()))
+    yield
+    for copy in across:
+        copy.wait_recv()
+
+
+def together(*gathers):
+    gathers = list(gathers)
+    while gathers:
+        for gather in list(gathers):
+            if next(gather, gathers) is gathers:
+                gathers.remove(gather)
+
+
+def plane_partners(here):
+    return [here.step(axis, way) for axis in ("x", "z") for way in (1, -1)]
+
+
+def column_partners(here):
+    return [here.step("y", 1), here.step("y", -1), here.other_core()]
+
+
+def small_gather(net, here, full, width):
+    def part(y):
+        return full.at[:, pl.ds(pl.multiple_of(here.column(y) * width, width), width)]
+
+    near = {way: net.send(part(here.y), here.step("y", way)) for way in (1, -1)}
+    across = [net.send(part(here.y), here.other_core())]
+    yield
+    near[1].wait_recv()
+    onward = net.send(part(ring(here.y, -1)), here.step("y", 1))
+    near[-1].wait_recv()
+    for way in (1, -1):
+        across.append(net.send(part(ring(here.y, -way)), here.other_core()))
+    yield
+    onward.wait_recv()
+    across.append(net.send(part(ring(here.y, 2)), here.other_core()))
+    yield
+    for copy in across:
+        copy.wait_recv()
+
+
+class Exchange:
+    def __init__(self, moves, sent, landed):
+        self.moves = []
+        for i, (source, target, to, keep) in enumerate(moves):
+            copy = pltpu.make_async_remote_copy(
+                src_ref=source,
+                dst_ref=target,
+                send_sem=sent.at[i],
+                recv_sem=landed.at[i],
+                device_id=to,
+                device_id_type=MESH,
+            )
+            local = pltpu.make_async_copy(source, target, landed.at[i])
+            self.moves.append((copy, local, keep))
+            if keep is None:
+                copy.start()
+            else:
+                pl.when(keep)(local.start)
+                pl.when(jnp.logical_not(keep))(copy.start)
+
+    def wait(self, i):
+        copy, local, keep = self.moves[i]
+        if keep is None:
+            copy.wait()
+        else:
+            pl.when(keep)(local.wait)
+            pl.when(jnp.logical_not(keep))(copy.wait)
+
+
+def weight_move(here, weight, full):
+    depth = weight.shape[0]
+    mine = pl.multiple_of((8 * here.z_lo + 2 * here.x + here.core) * depth, depth)
+    return weight, full.at[pl.ds(mine, depth), :], here.turned(), here.core == here.z_hi
+
+
+def weight_gather(net, here, full, depth):
+    half = depth // 2
+    return plane_gather(
+        net, here, full, half, lambda which, x, z: here.location(x, z) * depth + which * half
+    )
+
+
+def entry_kernel(tokens, gain, weight, tokens_full, gain_full, weight_full, sent, landed):
+    here = Place()
+    half_rows, width = tokens.shape[0] // 2, tokens.shape[1]
+    greet(
+        plane_partners(here)
+        + column_partners(here)
+        + [here.turned()]
+        + [here.chunk_to(half) for half in (0, 1)]
+        + [here.chunk_from(half) for half in (0, 1)]
+    )
+    columns = pl.ds(pl.multiple_of((2 * here.y + here.z_hi) * width, width), width)
+    rows_to = pl.ds(pl.multiple_of(here.core * half_rows, half_rows), half_rows)
+    landing = tokens_full.at[rows_to, columns]
+    stays = jnp.logical_and(here.core == 0, here.z_hi == 0)
+    first = Exchange(
+        [
+            weight_move(here, weight, weight_full),
+            (tokens.at[:half_rows, :], landing, here.chunk_to(0), stays),
+            (tokens.at[half_rows:, :], landing, here.chunk_to(1), None),
+            (gain, gain_full.at[:, columns], here.turned(), here.core == here.z_hi),
+        ],
+        sent,
+        landed,
+    )
+    net = Net(sent, landed, 4)
+    first.wait(0)
+    weights = weight_gather(net, here, weight_full, weight.shape[0])
+    next(weights)
+    first.wait(1)
+    first.wait(2)
+    features = column_gather(net, here, tokens_full, width)
+    next(features)
+    first.wait(3)
+    gains = small_gather(net, here, gain_full, width)
+    together(features, weights, gains)
+    net.finish()
+
+
+def keys_kernel(block, full, sent, landed, kept):
+    here = Place()
+    half_rows = block.shape[0] // 2
+    greet(plane_partners(here))
+    copies = []
+    for half in (0, 1):
+        start = pl.multiple_of(here.chunk(half, here.x, here.z) * half_rows, half_rows)
+        copies.append(
+            pltpu.make_async_copy(
+                block.at[half * half_rows : (half + 1) * half_rows, :],
+                full.at[pl.ds(start, half_rows), :],
+                kept.at[half],
+            )
+        )
+        copies[half].start()
+    net = Net(sent, landed)
+    together(
+        plane_gather(
+            net, here, full, half_rows,
+            lambda half, x, z: here.chunk(half, x, z) * half_rows,
+            own=lambda half: block.at[half * half_rows : (half + 1) * half_rows, :],
+        )
+    )
+    for copy in copies:
+        copy.wait()
+    net.finish()
+
+
+def heads_kernel(block, weight, full, weight_full, sent, landed, kept):
+    here = Place()
+    width = block.shape[1]
+    greet(plane_partners(here) + column_partners(here) + [here.turned()])
+    first = Exchange([weight_move(here, weight, weight_full)], sent, landed)
+    net = Net(sent, landed, 1)
+    start = pl.multiple_of(here.column() * width, width)
+    copy = pltpu.make_async_copy(block, full.at[:, pl.ds(start, width)], kept.at[0])
+    copy.start()
+    heads = column_gather(net, here, full, width, own=block)
+    next(heads)
+    first.wait(0)
+    together(weight_gather(net, here, weight_full, weight.shape[0]), heads)
+    copy.wait()
+    net.finish()
+
+
+def exit_kernel(block, home, sent, landed):
+    here = Place()
+    half_rows = block.shape[0] // 2
+    greet([f(half) for f in (here.chunk_to, here.chunk_from) for half in (0, 1)])
+    moves = []
+    for half in (0, 1):
+        slot = pl.multiple_of(((here.z_hi + half) % 2) * half_rows, half_rows)
+        stays = jnp.logical_and(here.core == 0, here.z_hi == 0) if half == 0 else None
+        moves.append(
+            (
+                block.at[pl.ds(slot, half_rows), :],
+                home.at[half * half_rows : (half + 1) * half_rows, :],
+                here.chunk_from(half),
+                stays,
+            )
+        )
+    last = Exchange(moves, sent, landed)
+    last.wait(0)
+    last.wait(1)
+
+
+PLANE, COLUMN, SMALL = 40, 11, 7
+
+
+def remote_call(kernel, number, copies, kept, shapes, *operands):
+    return pl.pallas_call(
+        kernel,
+        out_shape=[jax.ShapeDtypeStruct(shape, jnp.bfloat16) for shape in shapes],
+        in_specs=[pl.BlockSpec(memory_space=pl.ANY)] * len(operands),
+        out_specs=[pl.BlockSpec(memory_space=pl.ANY)] * len(shapes),
+        scratch_shapes=[
+            pltpu.SemaphoreType.DMA((copies,)),
+            pltpu.SemaphoreType.DMA((copies,)),
+        ]
+        + ([pltpu.SemaphoreType.DMA((kept,))] if kept else []),
+        compiler_params=pltpu.CompilerParams(collective_id=number, has_side_effects=True),
+        name=kernel.__name__,
+    )(*operands)
+
+
+def flash_kernel(scale, q_ref, kv_ref, o_ref, acc, top):
     rows = q_ref.shape[0]
     head_dim = kv_ref.shape[1] // 2
-    chunk = pl.program_id(0)
-    me = lax.axis_index("row")
-    index = jnp.where(chunk == 0, 2 * me, 2 * devices - 1 - 2 * me)
+    here = Place()
+    index = jnp.where(
+        pl.program_id(0) == 0, here.chunk(0, here.x, here.z), here.chunk(1, here.x, here.z)
+    )
     acc[...] = jnp.zeros_like(acc)
     top[...] = jnp.full_like(top, -1e30)
     factor_log2 = scale * math.log2(math.e)
@@ -84,12 +455,12 @@
         ).astype(o_ref.dtype)
 
 
-def flash(devices, scale, queries, keys_values):
+def flash(scale, queries, keys_values):
     rows, width = queries.shape
     half = rows // 2
     head_dim = width // GROUP
     return pl.pallas_call(
-        functools.partial(flash_kernel, devices, scale),
+        functools.partial(flash_kernel, scale),
         out_shape=jax.ShapeDtypeStruct(queries.shape, jnp.bfloat16),
         grid=(2,),
         in_specs=[
@@ -108,21 +479,40 @@
     )(queries, keys_values)
 
 
-def per_device(devices, tokens, norm_gain, qkv_weight, q_gain, k_gain, out_weight):
-    rows = tokens.shape[0]
+def rms_scale(values, gain):
+    mean_sq = jnp.mean(values * values, axis=-1, keepdims=True)
+    return values * lax.rsqrt(mean_sq + EPSILON) * gain
+
+
+def rotate(values, cosine, sine):
+    half = values.shape[-1] // 2
+    first = values[..., :half]
+    second = values[..., half:]
+    return jnp.concatenate(
+        [first * cosine - second * sine, second * cosine + first * sine], axis=-1
+    )
+
+
+def per_device(sizes, tokens, norm_gain, qkv_weight, q_gain, k_gain, out_weight):
+    n_row, n_col = sizes
+    rows, width = tokens.shape
     half = rows // 2
     head_dim = q_gain.shape[0]
-    tokens_full = lax.all_gather(tokens, "col", axis=1, tiled=True)
-    gain_full = lax.all_gather(norm_gain, "col", axis=0, tiled=True)
-    qkv_full = lax.all_gather(qkv_weight, "row", axis=0, tiled=True)
+    tokens_full, gain_full, qkv_full = remote_call(
+        entry_kernel, 1, 4 + PLANE + COLUMN + SMALL, 0,
+        [(rows, n_col * width), (16, n_col * width), (n_row * qkv_weight.shape[0], qkv_weight.shape[1])],
+        tokens, jnp.broadcast_to(norm_gain[None, :], (16, width)), qkv_weight,
+    )
     widened = tokens_full.astype(jnp.float32)
     mean_sq = jnp.mean(widened * widened, axis=1, keepdims=True)
-    normed = (widened * lax.rsqrt(mean_sq + EPSILON) * gain_full.astype(jnp.float32)).astype(
-        jnp.bfloat16
-    )
+    normed = (
+        widened * lax.rsqrt(mean_sq + EPSILON) * gain_full[:1].astype(jnp.float32)
+    ).astype(jnp.bfloat16)
     projected = jnp.dot(normed, qkv_full, preferred_element_type=jnp.float32)
-    me = lax.axis_index("row")
-    positions = me * rows + jnp.arange(rows, dtype=jnp.int32)
+    here = Place()
+    chunks = [here.chunk(which, here.x, here.z) for which in (0, 1)]
+    within = jnp.arange(half, dtype=jnp.int32)
+    positions = jnp.concatenate([chunk * half + within for chunk in chunks])
     freqs = jnp.power(
         jnp.float32(ROPE_BASE),
         -jnp.arange(head_dim // 2, dtype=jnp.float32) * 2.0 / head_dim,
@@ -136,30 +526,27 @@
     )
     keys = rotate(rms_scale(pieces[GROUP], k_gain), cosine, sine).astype(jnp.bfloat16)
     values = pieces[GROUP + 1].astype(jnp.bfloat16)
-    swap = [(i, devices - 1 - i) for i in range(devices)]
-    keys_values = lax.all_gather(
-        jnp.concatenate([keys, values], axis=1), "row", axis=0, tiled=True
-    )
-    balanced = jnp.concatenate(
-        [queries[:half], lax.ppermute(queries[half:], "row", swap)], axis=0
-    )
-    attended = flash(devices, head_dim ** (-0.5), balanced, keys_values)
-    attended = jnp.concatenate(
-        [attended[:half], lax.ppermute(attended[half:], "row", swap)], axis=0
-    )
-    out_full = lax.all_gather(out_weight, "row", axis=0, tiled=True)
-    result = jnp.dot(
-        lax.all_gather(attended, "col", axis=1, tiled=True),
-        out_full,
-        preferred_element_type=jnp.float32,
-    )
-    return result.astype(jnp.bfloat16)
+    (keys_values,) = remote_call(
+        keys_kernel, 2, PLANE, 2, [(n_row * rows, 2 * head_dim)],
+        jnp.concatenate([keys, values], axis=1),
+    )
+    attended = flash(head_dim ** (-0.5), queries, keys_values)
+    attended_full, out_full = remote_call(
+        heads_kernel, 3, 1 + PLANE + COLUMN, 1,
+        [(rows, n_col * attended.shape[1]), (n_row * out_weight.shape[0], out_weight.shape[1])],
+        attended, out_weight,
+    )
+    result = jnp.dot(attended_full, out_full, preferred_element_type=jnp.float32)
+    (home,) = remote_call(
+        exit_kernel, 4, 2, 0, [(rows, out_weight.shape[1])], result.astype(jnp.bfloat16)
+    )
+    return home
 
 
 def solution(mesh):
     placed = (P("row", "col"), P("col"), P("row", "col"), P(), P(), P("row", "col"))
     return jax.shard_map(
-        functools.partial(per_device, mesh.shape["row"]),
+        functools.partial(per_device, (mesh.shape["row"], mesh.shape["col"])),
         mesh=mesh,
         in_specs=placed,
         out_specs=P("row", "col"),

time: 382 us -> 238 us (0.62)
  waiting for transfers between devices: 269 us -> 0 us
  Pallas kernels: 37.1 us -> 198 us
  blocking collectives: 27.2 us -> 0 us
  between operations: 13.3 us -> 0.16 us
  starting transfers between devices: 5.76 us -> 0 us
  local copies, waits for them, and re-layouts: 1.53 us -> 6.65 us
  other arithmetic: 11.2 us -> 16.3 us
    all_gather x5 -> x0, waiting for transfers between devices: 246 us -> none  [the longest x1 98.9 us: per_device(): lax.all_gather(attended, 'col', axis=1, tiled=True)]
    pallas_call x1 -> x5, Pallas kernels: 37.1 us -> 198 us  [the longest x4 161 us: remote_call(): pl.pallas_call(kernel, out_shape=[jax.ShapeDtypeStruct(shape, jnp.bfloat1...]
    all_gather x1 -> x0, blocking collectives: 27.2 us -> none  [per_device(): gain_full = lax.all_gather(norm_gain, 'col', axis=0, tiled=True)]
    ppermute x2 -> x0, waiting for transfers between devices: 20.8 us -> none  [the longest x1 10.5 us: per_device(): lax.ppermute(queries[half:], 'row', swap)]
    ppermute x2 -> x0, starting transfers between devices: 5.6 us -> none  [the longest x1 2.8 us: per_device(): lax.ppermute(queries[half:], 'row', swap)]
  transfers between devices with their start and end apart: 7 -> 0, of which waited for: 6 -> 0; matrix products, arithmetic and copies ran while one was open for 2% -> 0% of each run, Pallas kernels for 10% -> 0%
where the time goes in v2:
time: 238 us
  Pallas kernels  198 us (83%)
  other arithmetic  16.3 us (7%)
  matrix products  16 us (7%)
  local copies, waits for them, and re-layouts  6.65 us (3%)
    pallas_call x4, Pallas kernels, remote_call(): pl.pallas_call(kernel, out_shape=[jax.ShapeDtypeStruct(shape, jnp.bfloat1...  161 us
    pallas_call x1, Pallas kernels, flash(): pl.pallas_call(functools.partial(flash_kernel, scale), out_shape=jax.Shap...  37.3 us
    dot_general x1, matrix products, per_device(): jnp.dot(attended_full, out_full, preferred_element_type=jnp.float32)  8.29 us
    dot_general x1, matrix products, per_device(): projected = jnp.dot(normed, qkv_full, preferred_element_type=jnp.float32)  7.69 us
    another operation x2, other arithmetic  7.06 us

profile of v2, /device:TPU:1, one launch (start us, length us, event | category | flops | bytes accessed | tf_op | source)
XLA Modules:
  0.0 237.6 jit_solution(197621635697317225)
XLA Ops:
  0.0 1.3 broadcast_in_dim.2.gain
  1.3 71.8 %entry_kernel.1 = (bf16[768,4096]{1,0:T(8,128)(2,1)}, bf16[16,4096]{1,0:T(8,128)(2,1)}, bf16[4096,768]{1,0:T(8,128)(2,1)}) custom-call(bf16[768,512]{1,0:T(8,128)(2,1)} %tokens.1, bf16[16,512]{1,0:T(8,128)(2,1)} %broadcast_in_dim.2.gain, bf16[256,768]{1,0:T(8,128)(2,1)} %weight.2), custom_call_target="tpu_custom_call" | custom-call | tf_op jit(solution)/shard_map/entry_kernel/pallas_call | solution.py:387
  73.1 0.0 copy-start.1
  73.1 1.0 slice_convert_fusion.1
  74.1 4.3 %fusion = f32[768]{0:T(1024)S(1)} fusion(bf16[768,4096]{1,0:T(8,128)(2,1)} %get-tuple-element.10), kind=kLoop, calls=%fused_computation.2 | loop fusion | flops 9436416 | bytes 6294528 | tf_op jit(solution)/shard_map/reduce_sum | solution.py:507
  78.4 0.0 copy-done.1
  78.4 0.0 copy-start.2
  78.4 0.0 copy-start.3
  78.4 7.7 %fusion.3 = f32[768,768]{1,0:T(8,128)S(1)} fusion(bf16[4096,768]{1,0:T(8,128)(2,1)} %get-tuple-element.12, bf16[768,4096]{1,0:T(8,128)(2,1)S(1)} %copy-done.1, f32[4096]{0:T(1024)S(1)} %bitcast.4, f32[768]{0:T(1024)S(1)} %add_rsqrt_fusion.5), kind=kOutput, calls=%fused_computation.5 | convolution fusion | flops 4844421120 | bytes 14961664 | tf_op jit(solution)/shard_map/dot_general | solution.py:511
  86.1 0.6 multiply_reduce_fusion
  86.8 0.0 copy-done.2
  86.8 0.0 copy-done.3
  86.8 1.4 multiply_multiply_fusion.1
  88.2 2.5 %fusion.30 = (bf16[768,64]{1,0:T(8,128)(2,1)}, bf16[768,64]{1,0:T(8,128)(2,1)}) fusion(f32[768,128]{1,0:T(8,128)S(1)} %get-tuple-element.21, f32[768]{0:T(1024)S(1)} %add_convert_fusion, f32[64]{0:T(128)S(1)} %multiply_power_fusion), kind=kLoop, calls=%fused_computation.34 | loop fusion | flops 442368 | bytes 593152 | tf_op jit(solution)/shard_map/convert.11
  90.7 4.6 %fusion.44 = (bf16[768,64]{1,0:T(8,128)(2,1)}, bf16[768,64]{1,0:T(8,128)(2,1)}, bf16[768,64]{1,0:T(8,128)(2,1)S(1)}, bf16[768,64]{1,0:T(8,128)(2,1)S(1)}, bf16[7...) fusion(f32[768,128]{1,0:T(8,128)} %get-tuple-element.24, ...), kind=kLoop, calls=%fused_computation.48 | loop fusion | flops 1622016 | bytes 2362624 | tf_op jit(solution)/shard_map/convert.2
  95.3 2.4 %concatenate.26.q_ref = bf16[768,512]{1,0:T(8,128)(2,1)S(1)} concatenate(bf16[768,64]{1,0:T(8,128)(2,1)} %get-tuple-element.34, bf16[768,64]{1,0:T(8,128)(2,1)} %get-tuple-element.33, bf16[768,64]{1,0:T(8,128)(2,1)} %get-tuple-element.39, bf16[768,64]{1,0:T(8,128)(2,1)} %get-tuple-element.40, bf16[768,64]{1,0:T(8,128)(2,1)} %get-tuple-element.37, ...), dimensions={1} | concatenate | bytes 1572864 | tf_op jit(solution)/shard_map/concatenate | solution.py:523
  97.7 2.0 pad_maximum_fusion.block
  99.7 35.8 %keys_kernel.1.kv_ref = bf16[12288,256]{1,0:T(8,128)(2,1)} custom-call(bf16[768,256]{1,0:T(8,128)(2,1)} %pad_maximum_fusion.block), custom_call_target="tpu_custom_call" | custom-call | tf_op jit(solution)/shard_map/keys_kernel/pallas_call | solution.py:387
  135.5 37.3 %shard_map.64.block = bf16[768,512]{1,0:T(8,128)(2,1)S(1)} custom-call(bf16[768,512]{1,0:T(8,128)(2,1)S(1)} %concatenate.26.q_ref, bf16[12288,256]{1,0:T(8,128)(2,1)} %keys_kernel.1.kv_ref), custom_call_target="tpu_custom_call" | custom-call | flops 10000000000 | bytes 8000000 | tf_op jit(solution)/shard_map/pallas_call | solution.py:462
  172.8 0.0 copy-start
  172.8 0.9 copy-done
  173.7 38.9 %heads_kernel.1 = (bf16[768,4096]{1,0:T(8,128)(2,1)}, bf16[4096,512]{1,0:T(8,128)(2,1)}) custom-call(bf16[768,512]{1,0:T(8,128)(2,1)} %copy-done, bf16[256,512]{1,0:T(8,128)(2,1)} %weight.3), custom_call_target="tpu_custom_call" | custom-call | tf_op jit(solution)/shard_map/heads_kernel/pallas_call | solution.py:387
  212.7 8.3 %convolution_convert_fusion.block = bf16[768,512]{1,0:T(8,128)(2,1)} fusion(bf16[768,4096]{1,0:T(8,128)(2,1)} %get-tuple-element.13, bf16[4096,512]{1,0:T(8,128)(2,1)} %get-tuple-element.14), kind=kOutput, calls=%fused_computation.8 | convolution fusion | flops 3221618688 | bytes 11272192 | tf_op jit(solution)/shard_map/dot_general | solution.py:539
  220.9 14.5 %exit_kernel.1 = bf16[768,512]{1,0:T(8,128)(2,1)} custom-call(bf16[768,512]{1,0:T(8,128)(2,1)} %convolution_convert_fusion.block), custom_call_target="tpu_custom_call" | custom-call | tf_op jit(solution)/shard_map/exit_kernel/pallas_call | solution.py:387
  235.5 2.1 copy.22
  (8 shorter events, 0.1 us)
Async XLA Ops:
  73.1 5.3 %copy-start.1 = (bf16[768,4096]{1,0:T(8,128)(2,1)S(1)}, bf16[768,4096]{1,0:T(8,128)(2,1)}, u32[]{:S(2)}) copy-start(bf16[768,4096]{1,0:T(8,128)(2,1)} %get-tuple-element.10) | copy-start | bytes 18874372
  78.4 8.4 %copy-start.2 = (f32[128]{0:T(128)S(1)}, f32[128]{0:T(128)}, u32[]{:S(2)}) copy-start(f32[128]{0:T(128)} %param.9) | copy-start | bytes 1540
  78.4 8.4 %copy-start.3 = (f32[128]{0:T(128)S(1)}, f32[128]{0:T(128)}, u32[]{:S(2)}) copy-start(f32[128]{0:T(128)} %param.10) | copy-start | bytes 1540
  172.8 0.9 copy-start

commit v3 on v2

--- a/solution.py
+++ b/solution.py
@@ -12,7 +12,6 @@
 GROUP = 4
 EPSILON = 1e-06
 ROPE_BASE = 1000000.0
-KEY_BLOCK = 768
 MESH = pl.DeviceIdType.MESH
 
 
@@ -84,9 +83,37 @@
         self.copies.append(copy)
         return copy
 
+    def send_built(self, build):
+        copy = Built(self, self.base + len(self.copies), build)
+        copy.copy().start()
+        self.copies.append(copy)
+        return copy
+
     def finish(self):
         for copy in self.copies:
             copy.wait_send()
+
+
+class Built:
+    def __init__(self, net, i, build):
+        self.net, self.i, self.build = net, i, build
+
+    def copy(self):
+        ref, to, target = self.build()
+        return pltpu.make_async_remote_copy(
+            src_ref=ref,
+            dst_ref=target,
+            send_sem=self.net.sent.at[self.i],
+            recv_sem=self.net.landed.at[self.i],
+            device_id=to,
+            device_id_type=MESH,
+        )
+
+    def wait_recv(self):
+        self.copy().wait_recv()
+
+    def wait_send(self):
+        self.copy().wait_send()
 
 
 def greet(partners):
@@ -106,57 +133,66 @@
         return pl.multiple_of(spot(half, x, z), rows)
 
     def block(half, first, second):
-        return full.at[pl.ds(at(half, first, second), rows), :]
+        return full[half].at[pl.ds(at(half, first, second), rows), :]
 
     def part(half, first, second, way):
         start = at(half, first, second) + (0 if way == 1 else piece)
-        return full.at[pl.ds(pl.multiple_of(start, piece), piece), :]
-
-    def mine(half):
-        return block(half, 0, 0) if own is None else own(half)
+        return full[half].at[pl.ds(pl.multiple_of(start, piece), piece), :]
+
+    def whole(half, where, way, axis=1):
+        def build():
+            target = block(half, where, 0)
+            source = own[half] if where == 0 and own is not None else target
+            return source, here.step(axes[half][axis], way), target
+
+        return net.send_built(build)
+
+    def share(half, first, second, way, axis):
+        def build():
+            ref = part(half, first, second, way)
+            return ref, here.step(axes[half][axis], way), ref
+
+        return net.send_built(build)
 
     one, two, onward, last = {}, {}, {}, {}
     both = [(half, way) for half in (0, 1) for way in (1, -1)]
     for half, way in both:
-        one[half, way] = net.send(
-            mine(half), here.step(axes[half][0], way), block(half, 0, 0)
-        )
-    for half, way in both:
-        two[half, 0, way] = net.send(
-            mine(half), here.step(axes[half][1], way), block(half, 0, 0)
-        )
+        one[half, way] = whole(half, 0, way, 0)
+    for half, way in both:
+        two[half, 0, way] = whole(half, 0, way)
     yield
     for half, way in both:
         one[half, way].wait_recv()
-        onward[half, way] = net.send(
-            part(half, -way, 0, way), here.step(axes[half][0], way)
-        )
+        onward[half, way] = share(half, -way, 0, way, 0)
     for half, way in both:
         for turn in (1, -1):
-            two[half, -way, turn] = net.send(
-                block(half, -way, 0), here.step(axes[half][1], turn)
-            )
-    yield
+            two[half, -way, turn] = whole(half, -way, turn)
     for half, way in both:
         two[half, 0, way].wait_recv()
-        last[half, 0, way] = net.send(
-            part(half, 0, -way, way), here.step(axes[half][1], way)
-        )
+        last[half, 0, way] = share(half, 0, -way, way, 1)
     yield
     for half, way in both:
         onward[half, way].wait_recv()
     for half, way in both:
-        two[half, 2, way] = net.send(block(half, 2, 0), here.step(axes[half][1], way))
-    yield
-    for where in (-1, 1, 2):
+        two[half, 2, way] = whole(half, 2, way)
+    yield
+    for where in (-1, 1):
         for half, way in both:
             two[half, where, way].wait_recv()
-            last[half, where, way] = net.send(
-                part(half, where, -way, way), here.step(axes[half][1], way)
-            )
-        yield
-    for copy in last.values():
-        copy.wait_recv()
+            last[half, where, way] = share(half, where, -way, way, 1)
+    yield
+    for half, way in both:
+        last[half, 0, way].wait_recv()
+    for half, way in both:
+        two[half, 2, way].wait_recv()
+        last[half, 2, way] = share(half, 2, -way, way, 1)
+    yield
+    for where in (-1, 1):
+        for half, way in both:
+            last[half, where, way].wait_recv()
+    yield
+    for half, way in both:
+        last[half, 2, way].wait_recv()
 
 
 def column_gather(net, here, full, width, own=None):
@@ -272,7 +308,8 @@
 def weight_gather(net, here, full, depth):
     half = depth // 2
     return plane_gather(
-        net, here, full, half, lambda which, x, z: here.location(x, z) * depth + which * half
+        net, here, (full, full), half,
+        lambda which, x, z: here.location(x, z) * depth + which * half,
     )
 
 
@@ -311,34 +348,6 @@
     first.wait(3)
     gains = small_gather(net, here, gain_full, width)
     together(features, weights, gains)
-    net.finish()
-
-
-def keys_kernel(block, full, sent, landed, kept):
-    here = Place()
-    half_rows = block.shape[0] // 2
-    greet(plane_partners(here))
-    copies = []
-    for half in (0, 1):
-        start = pl.multiple_of(here.chunk(half, here.x, here.z) * half_rows, half_rows)
-        copies.append(
-            pltpu.make_async_copy(
-                block.at[half * half_rows : (half + 1) * half_rows, :],
-                full.at[pl.ds(start, half_rows), :],
-                kept.at[half],
-            )
-        )
-        copies[half].start()
-    net = Net(sent, landed)
-    together(
-        plane_gather(
-            net, here, full, half_rows,
-            lambda half, x, z: here.chunk(half, x, z) * half_rows,
-            own=lambda half: block.at[half * half_rows : (half + 1) * half_rows, :],
-        )
-    )
-    for copy in copies:
-        copy.wait()
     net.finish()
 
 
@@ -399,98 +408,200 @@
     )(*operands)
 
 
-def flash_kernel(scale, q_ref, kv_ref, o_ref, acc, top):
-    rows = q_ref.shape[0]
-    head_dim = kv_ref.shape[1] // 2
+def attention_kernel(
+    scale, q_ref, k_ref, v_ref, o_ref, keys, values, acc, top, sent, landed
+):
+    rows, head_dim = k_ref.shape
+    half_rows = rows // 2
     here = Place()
-    index = jnp.where(
-        pl.program_id(0) == 0, here.chunk(0, here.x, here.z), here.chunk(1, here.x, here.z)
-    )
+    factor_log2 = scale * math.log2(math.e)
     acc[...] = jnp.zeros_like(acc)
     top[...] = jnp.full_like(top, -1e30)
-    factor_log2 = scale * math.log2(math.e)
-    ones = jnp.ones((KEY_BLOCK, head_dim), jnp.bfloat16)
-
-    def scores(h, keys):
-        return lax.dot_general(
-            q_ref[:, h * head_dim : (h + 1) * head_dim],
-            keys,
-            (((1,), (1,)), ((), ())),
-            preferred_element_type=jnp.float32,
+
+    def unit(which, key_parts, value_parts, allowed=None):
+        key_block = [ref[...] for ref in key_parts]
+        value_block = [ref[...] for ref in value_parts]
+        key_block = key_block[0] if len(key_block) == 1 else jnp.concatenate(key_block, axis=0)
+        value_block = (
+            value_block[0] if len(value_block) == 1 else jnp.concatenate(value_block, axis=0)
         )
-
-    def step(block, allowed):
-        start = pl.multiple_of(block * KEY_BLOCK, KEY_BLOCK)
-        keys = kv_ref[pl.ds(start, KEY_BLOCK), :head_dim]
-        values = kv_ref[pl.ds(start, KEY_BLOCK), head_dim:]
-        wide = jnp.concatenate([values, ones], axis=1)
-        following = scores(0, keys)
+        wide = jnp.concatenate([value_block, jnp.ones_like(value_block)], axis=1)
+        asked = q_ref.at[pl.ds(pl.multiple_of(which * half_rows, half_rows), half_rows), :]
+
+        def scores(h):
+            return lax.dot_general(
+                asked[:, h * head_dim : (h + 1) * head_dim],
+                key_block,
+                (((1,), (1,)), ((), ())),
+                preferred_element_type=jnp.float32,
+            )
+
+        following = scores(0)
         for h in range(GROUP):
             raw = following
             if h + 1 < GROUP:
-                following = scores(h + 1, keys)
+                following = scores(h + 1)
             if allowed is not None:
                 raw = jnp.where(allowed, raw, -1e30)
-            before = top[h]
+            before = top[which, h]
             now = jnp.maximum(before, jnp.max(raw, axis=-1, keepdims=True))
             shift = now[:, :1] * factor_log2
             weights = jnp.exp2(raw * factor_log2 - shift).astype(jnp.bfloat16)
             fade = jnp.exp2((before - now) * factor_log2)
             added = jnp.dot(weights, wide, preferred_element_type=jnp.float32)
-            acc[h] = acc[h] * jnp.concatenate([fade, fade], axis=1) + added
-            top[h] = now
-
-    full = index // 2
-
-    @pl.loop(0, full)
-    def _(block):
-        step(block, None)
-
-    key_pos = full * KEY_BLOCK + lax.broadcasted_iota(jnp.int32, (rows, KEY_BLOCK), 1)
-    query_pos = index * rows + lax.broadcasted_iota(jnp.int32, (rows, KEY_BLOCK), 0)
-    step(full, key_pos <= query_pos)
-    for h in range(GROUP):
-        o_ref[:, h * head_dim : (h + 1) * head_dim] = (
-            acc[h, :, :head_dim] / acc[h, :, head_dim:]
-        ).astype(o_ref.dtype)
-
-
-def flash(scale, queries, keys_values):
+            acc[which, h] = acc[which, h] * jnp.concatenate([fade, fade], axis=1) + added
+            top[which, h] = now
+
+    low, high = here.z_lo, 1 - here.z_lo
+
+    def low_chunk(x, z):
+        chunk = here.chunk(0, x, z)
+        return chunk + (z % 2) * (31 - 2 * chunk)
+
+    def part(full, x, z, which):
+        start = (4 * x + z) * rows + which * half_rows
+        return full.at[pl.ds(pl.multiple_of(start, half_rows), half_rows), :]
+
+    def at_once(places):
+        spots = [(ring(here.x, dx), ring(here.z, dz)) for dx, dz in places]
+        unit(
+            high,
+            [part(keys, x, z, z % 2) for x, z in spots],
+            [part(values, x, z, z % 2) for x, z in spots],
+        )
+        for x, z in spots:
+            before = (31 + low_chunk(here.x, here.z) - low_chunk(x, z)) // 32
+            which = high + before * (low - high)
+            theirs = 1 - z % 2 + before * (2 * (z % 2) - 1)
+            unit(which, [part(keys, x, z, theirs)], [part(values, x, z, theirs)])
+
+    greet(plane_partners(here))
+    net = Net(sent, landed)
+    arrivals = plane_gather(
+        net, here, (keys, values), rows, lambda half, x, z: (4 * x + z) * rows, (k_ref, v_ref)
+    )
+    next(arrivals)
+
+    def own(ref, which):
+        return ref.at[pl.ds(pl.multiple_of(which * half_rows, half_rows), half_rows), :]
+
+    square = (half_rows, half_rows)
+    allowed = lax.broadcasted_iota(jnp.int32, square, 1) <= lax.broadcasted_iota(
+        jnp.int32, square, 0
+    )
+    unit(low, [own(k_ref, low)], [own(v_ref, low)], allowed)
+    unit(high, [own(k_ref, high)], [own(v_ref, high)], allowed)
+    unit(high, [own(k_ref, low)], [own(v_ref, low)])
+    pairs = [
+        ((1, 0), (3, 0)), ((0, 1), (0, 3)), ((1, 1), (1, 3)), ((3, 1), (3, 3)),
+        ((2, 0), (0, 2)), ((2, 1), (2, 3)), ((1, 2), (3, 2)),
+    ]
+    steps = (0, 1, 2, 4, 5)
+
+    tables = tuple(
+        sum(pair[i][j] * 4**n for n, pair in enumerate(pairs)) for i in (0, 1) for j in (0, 1)
+    )
+
+    def stage(n, rest):
+        for when in steps:
+            pl.when(n == when)(lambda: next(arrivals) and None)
+        digits = [r % 4 for r in rest]
+        at_once([digits[:2], digits[2:]])
+        return tuple(r // 4 for r in rest)
+
+    lax.fori_loop(0, len(pairs), stage, tuple(jnp.int32(t) for t in tables))
+    next(arrivals, None)
+    at_once([(2, 2)])
+    net.finish()
+    for which in (0, 1):
+        for h in range(GROUP):
+            o_ref[
+                which * half_rows : (which + 1) * half_rows, h * head_dim : (h + 1) * head_dim
+            ] = (acc[which, h, :, :head_dim] / acc[which, h, :, head_dim:]).astype(o_ref.dtype)
+
+
+def attention(scale, places, queries, keys, values):
     rows, width = queries.shape
-    half = rows // 2
-    head_dim = width // GROUP
+    head_dim = keys.shape[1]
     return pl.pallas_call(
-        functools.partial(flash_kernel, scale),
+        functools.partial(attention_kernel, scale),
         out_shape=jax.ShapeDtypeStruct(queries.shape, jnp.bfloat16),
-        grid=(2,),
+        in_specs=[pl.BlockSpec(memory_space=pltpu.VMEM)] * 3,
+        out_specs=pl.BlockSpec(memory_space=pltpu.VMEM),
+        scratch_shapes=[
+            pltpu.VMEM((places * rows, head_dim), jnp.bfloat16),
+            pltpu.VMEM((places * rows, head_dim), jnp.bfloat16),
+            pltpu.VMEM((2, GROUP, rows // 2, 2 * head_dim), jnp.float32),
+            pltpu.VMEM((2, GROUP, rows // 2, head_dim), jnp.float32),
+            pltpu.SemaphoreType.DMA((PLANE,)),
+            pltpu.SemaphoreType.DMA((PLANE,)),
+        ],
+        compiler_params=pltpu.CompilerParams(
+            collective_id=2, has_side_effects=True, vmem_limit_bytes=48 * 1024 * 1024
+        ),
+        name="attention_kernel",
+    )(queries, keys, values)
+
+
+def project_kernel(
+    tokens, gain, weight, cosine, sine, q_gain, k_gain, q_ref, k_ref, v_ref
+):
+    rows, depth = tokens.shape
+    head_dim = k_ref.shape[1]
+    half = head_dim // 2
+    step = 512
+    spans = [slice(i, i + step) for i in range(0, depth, step)]
+    squares = jnp.zeros((rows, 128), jnp.float32)
+    for span in spans:
+        part = tokens[:, span].astype(jnp.float32)
+        part = part * part
+        for i in range(0, step, 128):
+            squares = squares + part[:, i : i + 128]
+    inverse = lax.rsqrt(jnp.sum(squares, axis=1, keepdims=True) / depth + EPSILON)
+    total = None
+    for span in spans:
+        part = tokens[:, span].astype(jnp.float32) * inverse
+        part = (part * gain[:1, span].astype(jnp.float32)).astype(jnp.bfloat16)
+        added = jnp.dot(part, weight[span, :], preferred_element_type=jnp.float32)
+        total = added if total is None else total + added
+    cos, sin = cosine[...], sine[...]
+
+    def turned(slot, head_gain):
+        u = total[:, slot * head_dim : (slot + 1) * head_dim]
+        mean_sq = jnp.mean(u * u, axis=-1, keepdims=True)
+        u = u * lax.rsqrt(mean_sq + EPSILON) * head_gain
+        return (u * cos + pltpu.roll(u, half, 1) * sin).astype(jnp.bfloat16)
+
+    for slot in range(GROUP):
+        q_ref[:, slot * head_dim : (slot + 1) * head_dim] = turned(slot, q_gain[...])
+    k_ref[...] = turned(GROUP, k_gain[...])
+    v_ref[...] = total[:, (GROUP + 1) * head_dim :].astype(jnp.bfloat16)
+
+
+def project(tokens, gain, weight, cosine, sine, q_gain, k_gain):
+    rows, depth = tokens.shape
+    head_dim = q_gain.shape[1]
+    block = rows // 4
+
+    def by_rows(width):
+        return pl.BlockSpec((block, width), lambda i: (i, 0))
+
+    def whole(array):
+        return pl.BlockSpec(array.shape, lambda i: (0, 0), pipeline_mode=pl.Buffered(1))
+
+    widths = [GROUP * head_dim, head_dim, head_dim]
+    return pl.pallas_call(
+        project_kernel,
+        out_shape=[jax.ShapeDtypeStruct((rows, w), jnp.bfloat16) for w in widths],
+        grid=(4,),
         in_specs=[
-            pl.BlockSpec((half, width), lambda i: (i, 0)),
-            pl.BlockSpec(keys_values.shape, lambda i: (0, 0), pipeline_mode=pl.Buffered(1)),
+            by_rows(depth), whole(gain), whole(weight), by_rows(head_dim), by_rows(head_dim),
+            whole(q_gain), whole(k_gain),
         ],
-        out_specs=pl.BlockSpec((half, width), lambda i: (i, 0)),
-        scratch_shapes=[
-            pltpu.VMEM((GROUP, half, 2 * head_dim), jnp.float32),
-            pltpu.VMEM((GROUP, half, head_dim), jnp.float32),
-        ],
-        compiler_params=pltpu.CompilerParams(vmem_limit_bytes=48 * 1024 * 1024),
-        cost_estimate=pl.CostEstimate(
-            flops=10_000_000_000, bytes_accessed=8_000_000, transcendentals=20_000_000
-        ),
-    )(queries, keys_values)
-
-
-def rms_scale(values, gain):
-    mean_sq = jnp.mean(values * values, axis=-1, keepdims=True)
-    return values * lax.rsqrt(mean_sq + EPSILON) * gain
-
-
-def rotate(values, cosine, sine):
-    half = values.shape[-1] // 2
-    first = values[..., :half]
-    second = values[..., half:]
-    return jnp.concatenate(
-        [first * cosine - second * sine, second * cosine + first * sine], axis=-1
-    )
+        out_specs=[by_rows(w) for w in widths],
+        compiler_params=pltpu.CompilerParams(vmem_limit_bytes=40 * 1024 * 1024),
+        name="project_kernel",
+    )(tokens, gain, weight, cosine, sine, q_gain, k_gain)
 
 
 def per_device(sizes, tokens, norm_gain, qkv_weight, q_gain, k_gain, out_weight):
@@ -503,12 +614,6 @@
         [(rows, n_col * width), (16, n_col * width), (n_row * qkv_weight.shape[0], qkv_weight.shape[1])],
         tokens, jnp.broadcast_to(norm_gain[None, :], (16, width)), qkv_weight,
     )
-    widened = tokens_full.astype(jnp.float32)
-    mean_sq = jnp.mean(widened * widened, axis=1, keepdims=True)
-    normed = (
-        widened * lax.rsqrt(mean_sq + EPSILON) * gain_full[:1].astype(jnp.float32)
-    ).astype(jnp.bfloat16)
-    projected = jnp.dot(normed, qkv_full, preferred_element_type=jnp.float32)
     here = Place()
     chunks = [here.chunk(which, here.x, here.z) for which in (0, 1)]
     within = jnp.arange(half, dtype=jnp.int32)
@@ -519,18 +624,16 @@
     )
     angles = positions.astype(jnp.float32)[:, None] * freqs[None, :]
     cosine, sine = jnp.cos(angles), jnp.sin(angles)
-    pieces = [projected[:, i * head_dim : (i + 1) * head_dim] for i in range(GROUP + 2)]
-    queries = jnp.concatenate(
-        [rotate(rms_scale(u, q_gain), cosine, sine).astype(jnp.bfloat16) for u in pieces[:GROUP]],
-        axis=1,
-    )
-    keys = rotate(rms_scale(pieces[GROUP], k_gain), cosine, sine).astype(jnp.bfloat16)
-    values = pieces[GROUP + 1].astype(jnp.bfloat16)
-    (keys_values,) = remote_call(
-        keys_kernel, 2, PLANE, 2, [(n_row * rows, 2 * head_dim)],
-        jnp.concatenate([keys, values], axis=1),
-    )
-    attended = flash(head_dim ** (-0.5), queries, keys_values)
+    queries, keys, values = project(
+        tokens_full,
+        gain_full,
+        qkv_full,
+        jnp.concatenate([cosine, cosine], axis=1),
+        jnp.concatenate([-sine, sine], axis=1),
+        q_gain[None, :],
+        k_gain[None, :],
+    )
+    attended = attention(head_dim ** (-0.5), n_row, queries, keys, values)
     attended_full, out_full = remote_call(
         heads_kernel, 3, 1 + PLANE + COLUMN, 1,
         [(rows, n_col * attended.shape[1]), (n_row * out_weight.shape[0], out_weight.shape[1])],

time: 238 us -> 200 us (0.84)
  Pallas kernels: 198 us -> 180 us
  other arithmetic: 16.3 us -> 1.81 us
  matrix products: 16 us -> 8.29 us
  local copies, waits for them, and re-layouts: 6.65 us -> 9.22 us
    pallas_call x4 -> x3, Pallas kernels: 161 us -> 121 us  [remote_call(): pl.pallas_call(kernel, out_shape=[jax.ShapeDtypeStruct(shape, jnp.bfloat1...]
    pallas_call x1 -> x2, Pallas kernels: 37.3 us -> 59.1 us  [the longest x1 47.6 us: attention(): pl.pallas_call(functools.partial(attention_kernel, scale), out_shape=jax....]
    dot_general x1 -> x0, matrix products: 7.69 us -> none  [per_device(): projected = jnp.dot(normed, qkv_full, preferred_element_type=jnp.float32)]
    another operation x2 -> x0, other arithmetic: 7.06 us -> none
    unnamed x9 -> x11, local copies, waits for them, and re-layouts: 2.95 us -> 7.93 us
    reduce_sum x2 -> x0, other arithmetic: 4.86 us -> none  [the longest x1 4.28 us: per_device(): mean_sq = jnp.mean(widened * widened, axis=1, keepdims=True)]
    mul x2 -> x0, other arithmetic: 2.42 us -> none  [the longest x1 1.42 us: rms_scale(): return values * lax.rsqrt(mean_sq + EPSILON) * gain]
    concatenate x1 -> x0, local copies, waits for them, and re-layouts: 2.38 us -> none  [per_device(): jnp.concatenate([rotate(rms_scale(u, q_gain), cosine, sine).astype(jnp.bf...]
where the time goes in v3:
time: 200 us; the launch traced here: 199 us
  Pallas kernels  180 us (90%)
  local copies, waits for them, and re-layouts  9.22 us (5%)
  matrix products  8.29 us (4%)
    pallas_call x3, Pallas kernels, remote_call(): pl.pallas_call(kernel, out_shape=[jax.ShapeDtypeStruct(shape, jnp.bfloat1...  121 us
    pallas_call x1, Pallas kernels, attention(): pl.pallas_call(functools.partial(attention_kernel, scale), out_shape=jax....  47.6 us
    pallas_call x1, Pallas kernels, project(): pl.pallas_call(project_kernel, out_shape=[jax.ShapeDtypeStruct((rows, w),...  11.6 us
    dot_general x1, matrix products, per_device(): jnp.dot(attended_full, out_full, preferred_element_type=jnp.float32)  8.29 us
    unnamed x11, local copies, waits for them, and re-layouts  7.93 us

profile of v3, /device:TPU:1, one launch (start us, length us, event | category | flops | bytes accessed | tf_op | source)
XLA Modules:
  0.0 199.4 jit_solution(4726053373359236497)
XLA Ops:
  0.0 1.3 broadcast_in_dim.6.gain
  1.3 1.4 fusion
  2.8 0.2 pad_maximum_fusion.1.sine
  3.0 0.2 pad_maximum_fusion.cosine
  3.1 65.9 %entry_kernel.1 = (bf16[768,4096]{1,0:T(8,128)(2,1)}, bf16[16,4096]{1,0:T(8,128)(2,1)}, bf16[4096,768]{1,0:T(8,128)(2,1)}) custom-call(bf16[768,512]{1,0:T(8,128)(2,1)} %tokens.1, bf16[16,512]{1,0:T(8,128)(2,1)} %broadcast_in_dim.6.gain, bf16[256,768]{1,0:T(8,128)(2,1)} %weight.2), custom_call_target="tpu_custom_call" | custom-call | tf_op jit(solution)/shard_map/entry_kernel/pallas_call | solution.py:396
  69.0 0.0 copy-start
  69.0 2.8 %copy-done = bf16[768,4096]{1,0:T(8,128)(2,1)S(1)} copy-done((bf16[768,4096]{1,0:T(8,128)(2,1)S(1)}, bf16[768,4096]{1,0:T(8,128)(2,1)}, u32[]{:S(2)}) %copy-start) | copy-done | bytes 6291480
  71.8 0.0 copy-start.2
  71.8 0.9 copy-done.2
  72.7 0.0 copy-start.3
  72.7 0.7 copy-done.3
  73.4 0.0 copy-start.4
  73.4 0.7 copy-done.4
  74.0 11.6 %project_kernel.1 = (bf16[768,512]{1,0:T(8,128)(2,1)S(1)}, bf16[768,128]{1,0:T(8,128)(2,1)S(1)}, bf16[768,128]{1,0:T(8,128)(2,1)S(1)}) custom-call(bf16[768,4096]{1,0:T(8,128)(2,1)S(1)} %copy-done, bf16[16,4096]{1,0:T(8,128)(2,1)S(1)} %copy-done.2, bf16[4096,768]{1,0:T(8,128)(2,1)} %get-tuple-element.15.weight, f32[768,128]{1,0:T(8,128)S(1)} %pad_maximum_fusion.cosine, ...), custom_call_target="tpu_custom_call" | custom-call | tf_op jit(solution)/shard_map/project_kernel/pallas_call | solution.py:593
  85.6 47.6 %attention_kernel.1.block = bf16[768,512]{1,0:T(8,128)(2,1)S(1)} custom-call(bf16[768,512]{1,0:T(8,128)(2,1)S(1)} %get-tuple-element.16.q_ref, bf16[768,128]{1,0:T(8,128)(2,1)S(1)} %get-tuple-element.17.k_ref, bf16[768,128]{1,0:T(8,128)(2,1)S(1)} %get-tuple-element.18.v_ref), custom_call_target="tpu_custom_call" | custom-call | tf_op jit(solution)/shard_map/attention_kernel/pallas_call | solution.py:526
  133.2 0.0 copy-start.1
  133.2 0.9 copy-done.1
  134.1 38.6 %heads_kernel.1 = (bf16[768,4096]{1,0:T(8,128)(2,1)}, bf16[4096,512]{1,0:T(8,128)(2,1)}) custom-call(bf16[768,512]{1,0:T(8,128)(2,1)} %copy-done.1, bf16[256,512]{1,0:T(8,128)(2,1)} %weight.3), custom_call_target="tpu_custom_call" | custom-call | tf_op jit(solution)/shard_map/heads_kernel/pallas_call | solution.py:396
  172.6 8.3 %convolution_convert_fusion.block = bf16[768,512]{1,0:T(8,128)(2,1)} fusion(bf16[768,4096]{1,0:T(8,128)(2,1)} %get-tuple-element.19, bf16[4096,512]{1,0:T(8,128)(2,1)} %get-tuple-element.20), kind=kOutput, calls=%fused_computation | convolution fusion | flops 3221618688 | bytes 11272192 | tf_op jit(solution)/shard_map/dot_general | solution.py:642
  180.9 16.4 %exit_kernel.1 = bf16[768,512]{1,0:T(8,128)(2,1)} custom-call(bf16[768,512]{1,0:T(8,128)(2,1)} %convolution_convert_fusion.block), custom_call_target="tpu_custom_call" | custom-call | tf_op jit(solution)/shard_map/exit_kernel/pallas_call | solution.py:396
  197.3 2.1 %copy.8 = bf16[768,512]{1,0:T(8,128)(2,1)} copy(bf16[768,512]{1,0:T(8,128)(2,1)} %exit_kernel.1) | data formatting | bytes 1572864
  (3 shorter events, 0.0 us)
Async XLA Ops:
  69.0 2.8 %copy-start = (bf16[768,4096]{1,0:T(8,128)(2,1)S(1)}, bf16[768,4096]{1,0:T(8,128)(2,1)}, u32[]{:S(2)}) copy-start(bf16[768,4096]{1,0:T(8,128)(2,1)} %get-tuple-element.13.tokens) | copy-start | bytes 18874372
  71.8 0.9 copy-start.2
  72.7 0.7 copy-start.3
  73.4 0.7 copy-start.4
  133.2 0.9 copy-start.1

commit v4 on v3

--- a/solution.py
+++ b/solution.py
@@ -195,27 +195,14 @@
         last[half, 2, way].wait_recv()
 
 
-def column_gather(net, here, full, width, own=None):
-    rows = full.shape[0]
-    piece = rows // 2
-
-    def part(y, which):
-        start = pl.multiple_of(here.column(y) * width, width)
-        rows_of = slice(which * piece, (which + 1) * piece) if which < 2 else slice(None)
-        return full.at[rows_of, pl.ds(start, width)]
-
-    def mine(which):
-        if own is None:
-            return part(here.y, which)
-        return own.at[slice(which * piece, (which + 1) * piece) if which < 2 else slice(None), :]
-
+def column_gather(net, here, part):
     far = {1: 0, -1: 1}
     near, onward, across = {}, {}, []
     for late in (0, 1):
         for way in (1, -1):
             which = far[way] if late == 0 else 1 - far[way]
-            near[way, late] = net.send(mine(which), here.step("y", way), part(here.y, which))
-    across.append(net.send(mine(2), here.other_core(), part(here.y, 2)))
+            near[way, late] = net.send(part(here.y, which), here.step("y", way))
+    across.append(net.send(part(here.y, 2), here.other_core()))
     yield
     for way in (1, -1):
         near[way, 0].wait_recv()
@@ -225,13 +212,21 @@
         near[way, 1].wait_recv()
         across.append(net.send(part(ring(here.y, -way), 2), here.other_core()))
     yield
-    yield
     for way in (1, -1):
         onward[way].wait_recv()
         across.append(net.send(part(ring(here.y, 2), far[way]), here.other_core()))
     yield
-    for copy in across:
-        copy.wait_recv()
+    across[0].wait_recv()
+    yield
+    across[1].wait_recv()
+    across[2].wait_recv()
+    yield
+    across[3].wait_recv()
+    across[4].wait_recv()
+
+
+def rows_of(rows, which):
+    return slice(None) if which == 2 else slice(which * (rows // 2), (which + 1) * (rows // 2))
 
 
 def together(*gathers):
@@ -271,9 +266,9 @@
 
 
 class Exchange:
-    def __init__(self, moves, sent, landed):
+    def __init__(self, moves, sent, landed, base=0):
         self.moves = []
-        for i, (source, target, to, keep) in enumerate(moves):
+        for i, (source, target, to, keep) in enumerate(moves, base):
             copy = pltpu.make_async_remote_copy(
                 src_ref=source,
                 dst_ref=target,
@@ -343,50 +338,17 @@
     next(weights)
     first.wait(1)
     first.wait(2)
-    features = column_gather(net, here, tokens_full, width)
+
+    def part(y, which):
+        start = pl.multiple_of(here.column(y) * width, width)
+        return tokens_full.at[rows_of(2 * half_rows, which), pl.ds(start, width)]
+
+    features = column_gather(net, here, part)
     next(features)
     first.wait(3)
     gains = small_gather(net, here, gain_full, width)
     together(features, weights, gains)
     net.finish()
-
-
-def heads_kernel(block, weight, full, weight_full, sent, landed, kept):
-    here = Place()
-    width = block.shape[1]
-    greet(plane_partners(here) + column_partners(here) + [here.turned()])
-    first = Exchange([weight_move(here, weight, weight_full)], sent, landed)
-    net = Net(sent, landed, 1)
-    start = pl.multiple_of(here.column() * width, width)
-    copy = pltpu.make_async_copy(block, full.at[:, pl.ds(start, width)], kept.at[0])
-    copy.start()
-    heads = column_gather(net, here, full, width, own=block)
-    next(heads)
-    first.wait(0)
-    together(weight_gather(net, here, weight_full, weight.shape[0]), heads)
-    copy.wait()
-    net.finish()
-
-
-def exit_kernel(block, home, sent, landed):
-    here = Place()
-    half_rows = block.shape[0] // 2
-    greet([f(half) for f in (here.chunk_to, here.chunk_from) for half in (0, 1)])
-    moves = []
-    for half in (0, 1):
-        slot = pl.multiple_of(((here.z_hi + half) % 2) * half_rows, half_rows)
-        stays = jnp.logical_and(here.core == 0, here.z_hi == 0) if half == 0 else None
-        moves.append(
-            (
-                block.at[pl.ds(slot, half_rows), :],
-                home.at[half * half_rows : (half + 1) * half_rows, :],
-                here.chunk_from(half),
-                stays,
-            )
-        )
-    last = Exchange(moves, sent, landed)
-    last.wait(0)
-    last.wait(1)
 
 
 PLANE, COLUMN, SMALL = 40, 11, 7
@@ -409,16 +371,35 @@
 
 
 def attention_kernel(
-    scale, q_ref, k_ref, v_ref, o_ref, keys, values, acc, top, sent, landed
+    scale, q_hbm, k_hbm, v_hbm, weight, home,
+    q_ref, k_ref, v_ref, keys, values, acc, top, heads, out_weight, total, result,
+    sent, landed, kept,
 ):
     rows, head_dim = k_ref.shape
     half_rows = rows // 2
     here = Place()
     factor_log2 = scale * math.log2(math.e)
+    loads = [
+        pltpu.make_async_copy(source, target, kept.at[i])
+        for i, (source, target) in enumerate(((k_hbm, k_ref), (v_hbm, v_ref), (q_hbm, q_ref)))
+    ]
+    for load in loads:
+        load.start()
+    greet(
+        plane_partners(here)
+        + column_partners(here)
+        + [here.turned()]
+        + [f(half) for f in (here.chunk_to, here.chunk_from) for half in (0, 1)]
+    )
+    net = Net(sent, landed, 3)
+    arrivals = plane_gather(
+        net, here, (keys, values), rows, lambda half, x, z: (4 * x + z) * rows, (k_hbm, v_hbm)
+    )
+    next(arrivals)
     acc[...] = jnp.zeros_like(acc)
     top[...] = jnp.full_like(top, -1e30)
 
-    def unit(which, key_parts, value_parts, allowed=None):
+    def unit(which, key_parts, value_parts, allowed=None, among=range(GROUP)):
         key_block = [ref[...] for ref in key_parts]
         value_block = [ref[...] for ref in value_parts]
         key_block = key_block[0] if len(key_block) == 1 else jnp.concatenate(key_block, axis=0)
@@ -436,10 +417,10 @@
                 preferred_element_type=jnp.float32,
             )
 
-        following = scores(0)
-        for h in range(GROUP):
+        following = scores(among[0])
+        for h in among:
             raw = following
-            if h + 1 < GROUP:
+            if h != among[-1]:
                 following = scores(h + 1)
             if allowed is not None:
                 raw = jnp.where(allowed, raw, -1e30)
@@ -462,29 +443,25 @@
         start = (4 * x + z) * rows + which * half_rows
         return full.at[pl.ds(pl.multiple_of(start, half_rows), half_rows), :]
 
-    def at_once(places):
+    def at_once(places, among=range(GROUP)):
         spots = [(ring(here.x, dx), ring(here.z, dz)) for dx, dz in places]
         unit(
             high,
             [part(keys, x, z, z % 2) for x, z in spots],
             [part(values, x, z, z % 2) for x, z in spots],
+            among=among,
         )
         for x, z in spots:
             before = (31 + low_chunk(here.x, here.z) - low_chunk(x, z)) // 32
             which = high + before * (low - high)
             theirs = 1 - z % 2 + before * (2 * (z % 2) - 1)
-            unit(which, [part(keys, x, z, theirs)], [part(values, x, z, theirs)])
-
-    greet(plane_partners(here))
-    net = Net(sent, landed)
-    arrivals = plane_gather(
-        net, here, (keys, values), rows, lambda half, x, z: (4 * x + z) * rows, (k_ref, v_ref)
-    )
-    next(arrivals)
+            unit(which, [part(keys, x, z, theirs)], [part(values, x, z, theirs)], among=among)
 
     def own(ref, which):
         return ref.at[pl.ds(pl.multiple_of(which * half_rows, half_rows), half_rows), :]
 
+    for load in loads:
+        load.wait()
     square = (half_rows, half_rows)
     allowed = lax.broadcasted_iota(jnp.int32, square, 1) <= lax.broadcasted_iota(
         jnp.int32, square, 0
@@ -494,7 +471,7 @@
     unit(high, [own(k_ref, low)], [own(v_ref, low)])
     pairs = [
         ((1, 0), (3, 0)), ((0, 1), (0, 3)), ((1, 1), (1, 3)), ((3, 1), (3, 3)),
-        ((2, 0), (0, 2)), ((2, 1), (2, 3)), ((1, 2), (3, 2)),
+        ((2, 0), (0, 2)), ((2, 1), (2, 3)),
     ]
     steps = (0, 1, 2, 4, 5)
 
@@ -510,37 +487,121 @@
         return tuple(r // 4 for r in rest)
 
     lax.fori_loop(0, len(pairs), stage, tuple(jnp.int32(t) for t in tables))
+
+    turn = Exchange([weight_move(here, weight, out_weight)], sent, landed)
     next(arrivals, None)
-    at_once([(2, 2)])
+    spread, weights = [], None
+    for h in range(GROUP):
+        at_once([(1, 2), (3, 2)], [h])
+        at_once([(2, 2)], [h])
+        for which in (0, 1):
+            heads[here.column() * GROUP + h, which * half_rows : (which + 1) * half_rows, :] = (
+                acc[which, h, :, :head_dim] / acc[which, h, :, head_dim:]
+            ).astype(heads.dtype)
+        spread.append(
+            column_gather(
+                net, here,
+                lambda y, which, h=h: heads.at[
+                    here.column(y) * GROUP + h, rows_of(rows, which), :
+                ],
+            )
+        )
+        next(spread[h])
+        if h == 1:
+            turn.wait(0)
+            weights = weight_gather(net, here, out_weight, weight.shape[0])
+            next(weights)
+    queue = [0, None, 1, 0, None, 2, 1, None, 3, 2, None, 3, 0, None, 1, 2, 3, None]
+    for h in queue:
+        next(weights if h is None else spread[h], None)
+
+    span = 2 * GROUP * head_dim
+    block = half_rows // 2
+
+    def product(y, start):
+        left = [
+            heads[2 * GROUP * y + i, pl.ds(pl.multiple_of(start, block), block), :]
+            for i in range(2 * GROUP)
+        ]
+        right = out_weight[pl.ds(pl.multiple_of(y * span, span), span), :]
+        return jnp.dot(
+            jnp.concatenate(left, axis=1), right, preferred_element_type=jnp.float32
+        )
+
+    for i, group in enumerate(((0,), (1, -1))):
+        for h in range(GROUP):
+            next(spread[h])
+        for shift in group:
+
+            @pl.loop(0, rows // block)
+            def _(n):
+                where = pl.ds(pl.multiple_of(n * block, block), block)
+                added = product(ring(here.y, shift), n * block)
+                total[where, :] = added if i == 0 else total[where, :] + added
+
+    for h in range(GROUP):
+        next(spread[h], None)
+    last = []
+    for half in (0, 1):
+        slot = pl.multiple_of(((here.z_hi + half) % 2) * half_rows, half_rows)
+
+        @pl.loop(0, half_rows // block)
+        def _(n):
+            start = slot + n * block
+            where = pl.ds(pl.multiple_of(start, block), block)
+            added = product(ring(here.y, 2), start)
+            result[where, :] = (total[where, :] + added).astype(result.dtype)
+
+        stays = jnp.logical_and(here.core == 0, here.z_hi == 0) if half == 0 else None
+        last.append(
+            Exchange(
+                [
+                    (
+                        result.at[pl.ds(slot, half_rows), :],
+                        home.at[half * half_rows : (half + 1) * half_rows, :],
+                        here.chunk_from(half),
+                        stays,
+                    )
+                ],
+                sent, landed, 1 + half,
+            )
+        )
+    for half in (0, 1):
+        last[half].wait(0)
     net.finish()
-    for which in (0, 1):
-        for h in range(GROUP):
-            o_ref[
-                which * half_rows : (which + 1) * half_rows, h * head_dim : (h + 1) * head_dim
-            ] = (acc[which, h, :, :head_dim] / acc[which, h, :, head_dim:]).astype(o_ref.dtype)
-
-
-def attention(scale, places, queries, keys, values):
+
+
+def attention(scale, places, columns, queries, keys, values, weight):
     rows, width = queries.shape
     head_dim = keys.shape[1]
+    copies = 3 + 2 * PLANE + GROUP * COLUMN
+    bf16, f32 = jnp.bfloat16, jnp.float32
     return pl.pallas_call(
         functools.partial(attention_kernel, scale),
-        out_shape=jax.ShapeDtypeStruct(queries.shape, jnp.bfloat16),
-        in_specs=[pl.BlockSpec(memory_space=pltpu.VMEM)] * 3,
-        out_specs=pl.BlockSpec(memory_space=pltpu.VMEM),
+        out_shape=jax.ShapeDtypeStruct((rows, weight.shape[1]), bf16),
+        in_specs=[pl.BlockSpec(memory_space=pl.ANY)] * 4,
+        out_specs=pl.BlockSpec(memory_space=pl.ANY),
         scratch_shapes=[
-            pltpu.VMEM((places * rows, head_dim), jnp.bfloat16),
-            pltpu.VMEM((places * rows, head_dim), jnp.bfloat16),
-            pltpu.VMEM((2, GROUP, rows // 2, 2 * head_dim), jnp.float32),
-            pltpu.VMEM((2, GROUP, rows // 2, head_dim), jnp.float32),
-            pltpu.SemaphoreType.DMA((PLANE,)),
-            pltpu.SemaphoreType.DMA((PLANE,)),
+            pltpu.VMEM(queries.shape, bf16),
+            pltpu.VMEM(keys.shape, bf16),
+            pltpu.VMEM(values.shape, bf16),
+            pltpu.VMEM((places * rows, head_dim), bf16),
+            pltpu.VMEM((places * rows, head_dim), bf16),
+            pltpu.VMEM((2, GROUP, rows // 2, 2 * head_dim), f32),
+            pltpu.VMEM((2, GROUP, rows // 2, head_dim), f32),
+            pltpu.VMEM((columns * GROUP, rows, head_dim), bf16),
+            pltpu.VMEM((places * weight.shape[0], weight.shape[1]), bf16),
+            pltpu.VMEM((rows, weight.shape[1]), f32),
+            pltpu.VMEM((rows, weight.shape[1]), bf16),
+            pltpu.SemaphoreType.DMA((copies,)),
+            pltpu.SemaphoreType.DMA((copies,)),
+            pltpu.SemaphoreType.DMA((3,)),
         ],
         compiler_params=pltpu.CompilerParams(
             collective_id=2, has_side_effects=True, vmem_limit_bytes=48 * 1024 * 1024
         ),
         name="attention_kernel",
-    )(queries, keys, values)
+    )(queries, keys, values, weight)
 
 
 def project_kernel(
@@ -633,17 +694,7 @@
         q_gain[None, :],
         k_gain[None, :],
     )
-    attended = attention(head_dim ** (-0.5), n_row, queries, keys, values)
-    attended_full, out_full = remote_call(
-        heads_kernel, 3, 1 + PLANE + COLUMN, 1,
-        [(rows, n_col * attended.shape[1]), (n_row * out_weight.shape[0], out_weight.shape[1])],
-        attended, out_weight,
-    )
-    result = jnp.dot(attended_full, out_full, preferred_element_type=jnp.float32)
-    (home,) = remote_call(
-        exit_kernel, 4, 2, 0, [(rows, out_weight.shape[1])], result.astype(jnp.bfloat16)
-    )
-    return home
+    return attention(head_dim ** (-0.5), n_row, n_col, queries, keys, values, out_weight)
 
 
 def solution(mesh):

time: 200 us -> 182 us (0.910)
  matrix products: 8.29 us -> 0 us
  Pallas kernels: 180 us -> 173 us
  local copies, waits for them, and re-layouts: 9.22 us -> 7.17 us
    pallas_call x3 -> x1, Pallas kernels: 121 us -> 64.8 us  [remote_call(): pl.pallas_call(kernel, out_shape=[jax.ShapeDtypeStruct(shape, jnp.bfloat1...]
    pallas_call x1, Pallas kernels: 47.6 us -> 96.4 us  [attention(): pl.pallas_call(functools.partial(attention_kernel, scale), out_shape=jax....]
    dot_general x1 -> x0, matrix products: 8.29 us -> none  [per_device(): jnp.dot(attended_full, out_full, preferred_element_type=jnp.float32)]
    unnamed x11, local copies, waits for them, and re-layouts: 7.93 us -> 5.88 us
where the time goes in v4:
time: 182 us
  Pallas kernels  173 us (95%)
  local copies, waits for them, and re-layouts  7.17 us (4%)
    pallas_call x1, Pallas kernels, attention(): pl.pallas_call(functools.partial(attention_kernel, scale), out_shape=jax....  96.4 us
    pallas_call x1, Pallas kernels, remote_call(): pl.pallas_call(kernel, out_shape=[jax.ShapeDtypeStruct(shape, jnp.bfloat1...  64.8 us
    pallas_call x1, Pallas kernels, project(): pl.pallas_call(project_kernel, out_shape=[jax.ShapeDtypeStruct((rows, w),...  11.6 us
    unnamed x11, local copies, waits for them, and re-layouts  5.88 us

profile of v4, /device:TPU:1, one launch (start us, length us, event | category | flops | bytes accessed | tf_op | source)
XLA Modules:
  0.0 181.9 jit_solution(13969961586363749382)
XLA Ops:
  0.0 1.3 broadcast_in_dim.6.gain
  1.3 1.4 fusion
  2.8 0.2 pad_maximum_fusion.1.sine
  3.0 0.2 pad_maximum_fusion.cosine
  3.1 64.8 %entry_kernel.1 = (bf16[768,4096]{1,0:T(8,128)(2,1)}, bf16[16,4096]{1,0:T(8,128)(2,1)}, bf16[4096,768]{1,0:T(8,128)(2,1)}) custom-call(bf16[768,512]{1,0:T(8,128)(2,1)} %tokens.1, bf16[16,512]{1,0:T(8,128)(2,1)} %broadcast_in_dim.6.gain, bf16[256,768]{1,0:T(8,128)(2,1)} %weight.2), custom_call_target="tpu_custom_call" | custom-call | tf_op jit(solution)/shard_map/entry_kernel/pallas_call | solution.py:358
  68.0 0.0 copy-start
  68.0 2.8 %copy-done = bf16[768,4096]{1,0:T(8,128)(2,1)S(1)} copy-done((bf16[768,4096]{1,0:T(8,128)(2,1)S(1)}, bf16[768,4096]{1,0:T(8,128)(2,1)}, u32[]{:S(2)}) %copy-start) | copy-done | bytes 6291480
  70.8 0.0 copy-start.2
  70.8 0.9 copy-done.2
  71.7 0.0 copy-start.3
  71.7 0.7 copy-done.3
  72.3 0.0 copy-start.4
  72.3 0.7 copy-done.4
  73.0 0.0 copy-start.1
  73.0 11.6 %project_kernel.1 = (bf16[768,512]{1,0:T(8,128)(2,1)S(1)}, bf16[768,128]{1,0:T(8,128)(2,1)S(1)}, bf16[768,128]{1,0:T(8,128)(2,1)S(1)}) custom-call(bf16[768,4096]{1,0:T(8,128)(2,1)S(1)} %copy-done, bf16[16,4096]{1,0:T(8,128)(2,1)S(1)} %copy-done.2, bf16[4096,768]{1,0:T(8,128)(2,1)} %get-tuple-element.13.weight, f32[768,128]{1,0:T(8,128)S(1)} %pad_maximum_fusion.cosine, ...), custom_call_target="tpu_custom_call" | custom-call | tf_op jit(solution)/shard_map/project_kernel/pallas_call | solution.py:654
  84.6 0.0 copy-done.1
  84.6 96.4 %attention_kernel.1 = bf16[768,512]{1,0:T(8,128)(2,1)S(1)} custom-call(bf16[768,512]{1,0:T(8,128)(2,1)S(1)} %get-tuple-element.14.q_hbm, bf16[768,128]{1,0:T(8,128)(2,1)S(1)} %get-tuple-element.15.k_hbm, bf16[768,128]{1,0:T(8,128)(2,1)S(1)} %get-tuple-element.16.v_hbm, bf16[256,512]{1,0:T(8,128)(2,1)S(1)} %copy-done.1), custom_call_target="tpu_custom_call" | custom-call | tf_op jit(solution)/shard_map/attention_kernel/pallas_call | solution.py:579
  181.0 0.9 copy.8
  (3 shorter events, 0.0 us)
Async XLA Ops:
  68.0 2.8 %copy-start = (bf16[768,4096]{1,0:T(8,128)(2,1)S(1)}, bf16[768,4096]{1,0:T(8,128)(2,1)}, u32[]{:S(2)}) copy-start(bf16[768,4096]{1,0:T(8,128)(2,1)} %get-tuple-element.11.tokens) | copy-start | bytes 18874372
  70.8 0.9 copy-start.2
  71.7 0.7 copy-start.3
  72.3 0.7 copy-start.4
  73.0 11.6 %copy-start.1 = (bf16[256,512]{1,0:T(8,128)(2,1)S(1)}, bf16[256,512]{1,0:T(8,128)(2,1)}, u32[]{:S(2)}) copy-start(bf16[256,512]{1,0:T(8,128)(2,1)} %weight.3) | copy-start | bytes 786436

commit v5 on v4

--- a/solution.py
+++ b/solution.py
@@ -223,6 +223,29 @@
     yield
     across[3].wait_recv()
     across[4].wait_recv()
+
+
+def token_gather(net, here, part, arrived):
+    near, onward, across = {}, {}, []
+    for piece in (0, 1):
+        arrived(piece)
+        for way in (1, -1):
+            near[way, piece] = net.send(part(here.y, piece), here.step("y", way))
+        across.append(net.send(part(here.y, piece), here.other_core()))
+        yield
+    for piece in (0, 1):
+        for way in (1, -1):
+            near[way, piece].wait_recv()
+            if (way, piece) in ((1, 0), (-1, 1)):
+                onward[way] = net.send(part(ring(here.y, -way), piece), here.step("y", way))
+            across.append(net.send(part(ring(here.y, -way), piece), here.other_core()))
+        yield
+    for way, piece in ((1, 0), (-1, 1)):
+        onward[way].wait_recv()
+        across.append(net.send(part(ring(here.y, 2), piece), here.other_core()))
+    yield
+    for copy in across:
+        copy.wait_recv()
 
 
 def rows_of(rows, which):
@@ -308,23 +331,35 @@
     )
 
 
-def entry_kernel(tokens, gain, weight, tokens_full, gain_full, weight_full, sent, landed):
+PLANE, TOKEN, COLUMN, SMALL = 40, 14, 11, 7
+SINGLE = 7
+
+
+def layer_kernel(
+    scale, tokens, gain, qkv_weight, weight, cosine, sine, q_gain, k_gain, home,
+    tokens_full, gain_full, qkv_full, normed,
+    q_ref, k_ref, v_ref, keys, values, acc, top, heads, out_weight, total, result,
+    sent, landed,
+):
+    rows, head_dim = k_ref.shape
+    half_rows = rows // 2
+    width, depth = tokens.shape[1], tokens_full.shape[1]
     here = Place()
-    half_rows, width = tokens.shape[0] // 2, tokens.shape[1]
+    factor_log2 = scale * math.log2(math.e)
     greet(
         plane_partners(here)
         + column_partners(here)
         + [here.turned()]
-        + [here.chunk_to(half) for half in (0, 1)]
-        + [here.chunk_from(half) for half in (0, 1)]
-    )
+        + [f(half) for f in (here.chunk_to, here.chunk_from) for half in (0, 1)]
+    )
+
     columns = pl.ds(pl.multiple_of((2 * here.y + here.z_hi) * width, width), width)
     rows_to = pl.ds(pl.multiple_of(here.core * half_rows, half_rows), half_rows)
     landing = tokens_full.at[rows_to, columns]
     stays = jnp.logical_and(here.core == 0, here.z_hi == 0)
     first = Exchange(
         [
-            weight_move(here, weight, weight_full),
+            weight_move(here, qkv_weight, qkv_full),
             (tokens.at[:half_rows, :], landing, here.chunk_to(0), stays),
             (tokens.at[half_rows:, :], landing, here.chunk_to(1), None),
             (gain, gain_full.at[:, columns], here.turned(), here.core == here.z_hi),
@@ -332,70 +367,74 @@
         sent,
         landed,
     )
-    net = Net(sent, landed, 4)
+    net = Net(sent, landed, SINGLE)
+
+    def token_part(y, piece):
+        slot = pl.multiple_of(((here.z_hi + piece) % 2) * half_rows, half_rows)
+        start = pl.multiple_of(here.column(y) * width, width)
+        return tokens_full.at[pl.ds(slot, half_rows), pl.ds(start, width)]
+
     first.wait(0)
-    weights = weight_gather(net, here, weight_full, weight.shape[0])
+    weights = weight_gather(net, here, qkv_full, qkv_weight.shape[0])
     next(weights)
-    first.wait(1)
-    first.wait(2)
-
-    def part(y, which):
-        start = pl.multiple_of(here.column(y) * width, width)
-        return tokens_full.at[rows_of(2 * half_rows, which), pl.ds(start, width)]
-
-    features = column_gather(net, here, part)
+    features = token_gather(net, here, token_part, lambda piece: first.wait(1 + piece))
+    next(features)
     next(features)
     first.wait(3)
-    gains = small_gather(net, here, gain_full, width)
-    together(features, weights, gains)
-    net.finish()
-
-
-PLANE, COLUMN, SMALL = 40, 11, 7
-
-
-def remote_call(kernel, number, copies, kept, shapes, *operands):
-    return pl.pallas_call(
-        kernel,
-        out_shape=[jax.ShapeDtypeStruct(shape, jnp.bfloat16) for shape in shapes],
-        in_specs=[pl.BlockSpec(memory_space=pl.ANY)] * len(operands),
-        out_specs=[pl.BlockSpec(memory_space=pl.ANY)] * len(shapes),
-        scratch_shapes=[
-            pltpu.SemaphoreType.DMA((copies,)),
-            pltpu.SemaphoreType.DMA((copies,)),
-        ]
-        + ([pltpu.SemaphoreType.DMA((kept,))] if kept else []),
-        compiler_params=pltpu.CompilerParams(collective_id=number, has_side_effects=True),
-        name=kernel.__name__,
-    )(*operands)
-
-
-def attention_kernel(
-    scale, q_hbm, k_hbm, v_hbm, weight, home,
-    q_ref, k_ref, v_ref, keys, values, acc, top, heads, out_weight, total, result,
-    sent, landed, kept,
-):
-    rows, head_dim = k_ref.shape
-    half_rows = rows // 2
-    here = Place()
-    factor_log2 = scale * math.log2(math.e)
-    loads = [
-        pltpu.make_async_copy(source, target, kept.at[i])
-        for i, (source, target) in enumerate(((k_hbm, k_ref), (v_hbm, v_ref), (q_hbm, q_ref)))
-    ]
-    for load in loads:
-        load.start()
-    greet(
-        plane_partners(here)
-        + column_partners(here)
-        + [here.turned()]
-        + [f(half) for f in (here.chunk_to, here.chunk_from) for half in (0, 1)]
-    )
-    net = Net(sent, landed, 3)
+    together(features, weights, small_gather(net, here, gain_full, width))
+
+    step, span = 64, 512
+    spans = [slice(i, i + span) for i in range(0, depth, span)]
+
+    @pl.loop(0, rows // step)
+    def _(n):
+        where = pl.ds(pl.multiple_of(n * step, step), step)
+        squares = jnp.zeros((step, 128), jnp.float32)
+        for cut in spans:
+            part = tokens_full[where, cut].astype(jnp.float32)
+            part = part * part
+            for i in range(0, span, 128):
+                squares = squares + part[:, i : i + 128]
+        inverse = lax.rsqrt(jnp.sum(squares, axis=1, keepdims=True) / depth + EPSILON)
+        for cut in spans:
+            part = tokens_full[where, cut].astype(jnp.float32) * inverse
+            normed[where, cut] = (part * gain_full[:1, cut].astype(jnp.float32)).astype(
+                normed.dtype
+            )
+
+    def turned(u, head_gain, where):
+        mean_sq = jnp.mean(u * u, axis=-1, keepdims=True)
+        u = u * lax.rsqrt(mean_sq + EPSILON) * head_gain
+        turn = pltpu.roll(u, head_dim // 2, 1)
+        return (u * cosine[where, :] + turn * sine[where, :]).astype(jnp.bfloat16)
+
+    block = half_rows // 2
+    q_width = GROUP * head_dim
+
+    @pl.loop(0, rows // block)
+    def _(n):
+        where = pl.ds(pl.multiple_of(n * block, block), block)
+        both = jnp.dot(
+            normed[where, :], qkv_full[:, q_width:], preferred_element_type=jnp.float32
+        )
+        k_ref[where, :] = turned(both[:, :head_dim], k_gain[...], where)
+        v_ref[where, :] = both[:, head_dim:].astype(v_ref.dtype)
+
     arrivals = plane_gather(
-        net, here, (keys, values), rows, lambda half, x, z: (4 * x + z) * rows, (k_hbm, v_hbm)
+        net, here, (keys, values), rows, lambda half, x, z: (4 * x + z) * rows, (k_ref, v_ref)
     )
     next(arrivals)
+
+    @pl.loop(0, rows // block)
+    def _(n):
+        where = pl.ds(pl.multiple_of(n * block, block), block)
+        four = jnp.dot(
+            normed[where, :], qkv_full[:, :q_width], preferred_element_type=jnp.float32
+        )
+        for h in range(GROUP):
+            cut = slice(h * head_dim, (h + 1) * head_dim)
+            q_ref[where, cut] = turned(four[:, cut], q_gain[...], where)
+
     acc[...] = jnp.zeros_like(acc)
     top[...] = jnp.full_like(top, -1e30)
 
@@ -460,8 +499,6 @@
     def own(ref, which):
         return ref.at[pl.ds(pl.multiple_of(which * half_rows, half_rows), half_rows), :]
 
-    for load in loads:
-        load.wait()
     square = (half_rows, half_rows)
     allowed = lax.broadcasted_iota(jnp.int32, square, 1) <= lax.broadcasted_iota(
         jnp.int32, square, 0
@@ -488,7 +525,7 @@
 
     lax.fori_loop(0, len(pairs), stage, tuple(jnp.int32(t) for t in tables))
 
-    turn = Exchange([weight_move(here, weight, out_weight)], sent, landed)
+    turn = Exchange([weight_move(here, weight, out_weight)], sent, landed, 4)
     next(arrivals, None)
     spread, weights = [], None
     for h in range(GROUP):
@@ -516,7 +553,6 @@
         next(weights if h is None else spread[h], None)
 
     span = 2 * GROUP * head_dim
-    block = half_rows // 2
 
     def product(y, start):
         left = [
@@ -563,106 +599,12 @@
                         stays,
                     )
                 ],
-                sent, landed, 1 + half,
+                sent, landed, 5 + half,
             )
         )
     for half in (0, 1):
         last[half].wait(0)
     net.finish()
-
-
-def attention(scale, places, columns, queries, keys, values, weight):
-    rows, width = queries.shape
-    head_dim = keys.shape[1]
-    copies = 3 + 2 * PLANE + GROUP * COLUMN
-    bf16, f32 = jnp.bfloat16, jnp.float32
-    return pl.pallas_call(
-        functools.partial(attention_kernel, scale),
-        out_shape=jax.ShapeDtypeStruct((rows, weight.shape[1]), bf16),
-        in_specs=[pl.BlockSpec(memory_space=pl.ANY)] * 4,
-        out_specs=pl.BlockSpec(memory_space=pl.ANY),
-        scratch_shapes=[
-            pltpu.VMEM(queries.shape, bf16),
-            pltpu.VMEM(keys.shape, bf16),
-            pltpu.VMEM(values.shape, bf16),
-            pltpu.VMEM((places * rows, head_dim), bf16),
-            pltpu.VMEM((places * rows, head_dim), bf16),
-            pltpu.VMEM((2, GROUP, rows // 2, 2 * head_dim), f32),
-            pltpu.VMEM((2, GROUP, rows // 2, head_dim), f32),
-            pltpu.VMEM((columns * GROUP, rows, head_dim), bf16),
-            pltpu.VMEM((places * weight.shape[0], weight.shape[1]), bf16),
-            pltpu.VMEM((rows, weight.shape[1]), f32),
-            pltpu.VMEM((rows, weight.shape[1]), bf16),
-            pltpu.SemaphoreType.DMA((copies,)),
-            pltpu.SemaphoreType.DMA((copies,)),
-            pltpu.SemaphoreType.DMA((3,)),
-        ],
-        compiler_params=pltpu.CompilerParams(
-            collective_id=2, has_side_effects=True, vmem_limit_bytes=48 * 1024 * 1024
-        ),
-        name="attention_kernel",
-    )(queries, keys, values, weight)
-
-
-def project_kernel(
-    tokens, gain, weight, cosine, sine, q_gain, k_gain, q_ref, k_ref, v_ref
-):
-    rows, depth = tokens.shape
-    head_dim = k_ref.shape[1]
-    half = head_dim // 2
-    step = 512
-    spans = [slice(i, i + step) for i in range(0, depth, step)]
-    squares = jnp.zeros((rows, 128), jnp.float32)
-    for span in spans:
-        part = tokens[:, span].astype(jnp.float32)
-        part = part * part
-        for i in range(0, step, 128):
-            squares = squares + part[:, i : i + 128]
-    inverse = lax.rsqrt(jnp.sum(squares, axis=1, keepdims=True) / depth + EPSILON)
-    total = None
-    for span in spans:
-        part = tokens[:, span].astype(jnp.float32) * inverse
-        part = (part * gain[:1, span].astype(jnp.float32)).astype(jnp.bfloat16)
-        added = jnp.dot(part, weight[span, :], preferred_element_type=jnp.float32)
-        total = added if total is None else total + added
-    cos, sin = cosine[...], sine[...]
-
-    def turned(slot, head_gain):
-        u = total[:, slot * head_dim : (slot + 1) * head_dim]
-        mean_sq = jnp.mean(u * u, axis=-1, keepdims=True)
-        u = u * lax.rsqrt(mean_sq + EPSILON) * head_gain
-        return (u * cos + pltpu.roll(u, half, 1) * sin).astype(jnp.bfloat16)
-
-    for slot in range(GROUP):
-        q_ref[:, slot * head_dim : (slot + 1) * head_dim] = turned(slot, q_gain[...])
-    k_ref[...] = turned(GROUP, k_gain[...])
-    v_ref[...] = total[:, (GROUP + 1) * head_dim :].astype(jnp.bfloat16)
-
-
-def project(tokens, gain, weight, cosine, sine, q_gain, k_gain):
-    rows, depth = tokens.shape
-    head_dim = q_gain.shape[1]
-    block = rows // 4
-
-    def by_rows(width):
-        return pl.BlockSpec((block, width), lambda i: (i, 0))
-
-    def whole(array):
-        return pl.BlockSpec(array.shape, lambda i: (0, 0), pipeline_mode=pl.Buffered(1))
-
-    widths = [GROUP * head_dim, head_dim, head_dim]
-    return pl.pallas_call(
-        project_kernel,
-        out_shape=[jax.ShapeDtypeStruct((rows, w), jnp.bfloat16) for w in widths],
-        grid=(4,),
-        in_specs=[
-            by_rows(depth), whole(gain), whole(weight), by_rows(head_dim), by_rows(head_dim),
-            whole(q_gain), whole(k_gain),
-        ],
-        out_specs=[by_rows(w) for w in widths],
-        compiler_params=pltpu.CompilerParams(vmem_limit_bytes=40 * 1024 * 1024),
-        name="project_kernel",
-    )(tokens, gain, weight, cosine, sine, q_gain, k_gain)
 
 
 def per_device(sizes, tokens, norm_gain, qkv_weight, q_gain, k_gain, out_weight):
@@ -670,11 +612,6 @@
     rows, width = tokens.shape
     half = rows // 2
     head_dim = q_gain.shape[0]
-    tokens_full, gain_full, qkv_full = remote_call(
-        entry_kernel, 1, 4 + PLANE + COLUMN + SMALL, 0,
-        [(rows, n_col * width), (16, n_col * width), (n_row * qkv_weight.shape[0], qkv_weight.shape[1])],
-        tokens, jnp.broadcast_to(norm_gain[None, :], (16, width)), qkv_weight,
-    )
     here = Place()
     chunks = [here.chunk(which, here.x, here.z) for which in (0, 1)]
     within = jnp.arange(half, dtype=jnp.int32)
@@ -685,16 +622,48 @@
     )
     angles = positions.astype(jnp.float32)[:, None] * freqs[None, :]
     cosine, sine = jnp.cos(angles), jnp.sin(angles)
-    queries, keys, values = project(
-        tokens_full,
-        gain_full,
-        qkv_full,
+    bf16, f32 = jnp.bfloat16, jnp.float32
+    copies = SINGLE + 3 * PLANE + TOKEN + SMALL + GROUP * COLUMN
+    q_width, out_width = GROUP * head_dim, out_weight.shape[1]
+    return pl.pallas_call(
+        functools.partial(layer_kernel, head_dim ** (-0.5)),
+        out_shape=jax.ShapeDtypeStruct((rows, out_width), bf16),
+        in_specs=[pl.BlockSpec(memory_space=pl.ANY)] * 4
+        + [pl.BlockSpec(memory_space=pltpu.VMEM)] * 4,
+        out_specs=pl.BlockSpec(memory_space=pl.ANY),
+        scratch_shapes=[
+            pltpu.VMEM((rows, n_col * width), bf16),
+            pltpu.VMEM((16, n_col * width), bf16),
+            pltpu.VMEM((n_row * qkv_weight.shape[0], qkv_weight.shape[1]), bf16),
+            pltpu.VMEM((rows, n_col * width), bf16),
+            pltpu.VMEM((rows, q_width), bf16),
+            pltpu.VMEM((rows, head_dim), bf16),
+            pltpu.VMEM((rows, head_dim), bf16),
+            pltpu.VMEM((n_row * rows, head_dim), bf16),
+            pltpu.VMEM((n_row * rows, head_dim), bf16),
+            pltpu.VMEM((2, GROUP, half, 2 * head_dim), f32),
+            pltpu.VMEM((2, GROUP, half, head_dim), f32),
+            pltpu.VMEM((n_col * GROUP, rows, head_dim), bf16),
+            pltpu.VMEM((n_row * out_weight.shape[0], out_width), bf16),
+            pltpu.VMEM((rows, out_width), f32),
+            pltpu.VMEM((rows, out_width), bf16),
+            pltpu.SemaphoreType.DMA((copies,)),
+            pltpu.SemaphoreType.DMA((copies,)),
+        ],
+        compiler_params=pltpu.CompilerParams(
+            collective_id=1, has_side_effects=True, vmem_limit_bytes=60 * 1024 * 1024
+        ),
+        name="layer_kernel",
+    )(
+        tokens,
+        jnp.broadcast_to(norm_gain[None, :], (16, width)),
+        qkv_weight,
+        out_weight,
         jnp.concatenate([cosine, cosine], axis=1),
         jnp.concatenate([-sine, sine], axis=1),
         q_gain[None, :],
         k_gain[None, :],
     )
-    return attention(head_dim ** (-0.5), n_row, n_col, queries, keys, values, out_weight)
 
 
 def solution(mesh):

time: 182 us -> 165 us (0.907)
  Pallas kernels: 173 us -> 158 us
  local copies, waits for them, and re-layouts: 7.17 us -> 3.33 us
    pallas_call x3 -> x1, Pallas kernels: 173 us -> 158 us  [per_device(): pl.pallas_call(functools.partial(layer_kernel, head_dim ** (-0.5)), out_s...]
    unnamed x11 -> x3, local copies, waits for them, and re-layouts: 5.88 us -> 2.72 us
where the time goes in v5:
time: 165 us; the launch traced here: 164 us
  Pallas kernels  158 us (96%)
  local copies, waits for them, and re-layouts  3.33 us (2%)
  other arithmetic  3.3 us (2%)
    pallas_call x1, Pallas kernels, per_device(): pl.pallas_call(functools.partial(layer_kernel, head_dim ** (-0.5)), out_s...  158 us

profile of v5, /device:TPU:1, one launch (start us, length us, event | category | flops | bytes accessed | tf_op | source)
XLA Modules:
  0.0 164.4 jit_solution(7136142256488564205)
XLA Ops:
  0.0 0.0 copy-start
  0.1 0.7 copy-done
  0.7 0.6 broadcast_in_dim.6.gain
  1.3 1.4 fusion
  2.8 0.9 pad_maximum_fusion.1.sine
  3.7 0.9 pad_maximum_fusion.cosine
  4.6 157.8 %layer_kernel.1 = bf16[768,512]{1,0:T(8,128)(2,1)} custom-call(bf16[768,512]{1,0:T(8,128)(2,1)} %tokens.1, bf16[16,512]{1,0:T(8,128)(2,1)} %broadcast_in_dim.6.gain, bf16[256,768]{1,0:T(8,128)(2,1)} %qkv_weight.1, bf16[256,512]{1,0:T(8,128)(2,1)} %weight.1, f32[768,128]{1,0:T(8,128)} %pad_maximum_fusion.cosine, f32[768,128]{1,0:T(8,128)} %pad_maximum_fusion.1.sine, ...), custom_call_target="tpu_custom_call" | custom-call | tf_op jit(solution)/shard_map/layer_kernel/pallas_call | solution.py:628
  162.4 2.1 %copy.8 = bf16[768,512]{1,0:T(8,128)(2,1)} copy(bf16[768,512]{1,0:T(8,128)(2,1)} %layer_kernel.1) | data formatting | bytes 1572864
  (3 shorter events, 0.0 us)
Async XLA Ops:
  0.0 0.7 copy-start

commit v6 on v5

--- a/solution.py
+++ b/solution.py
@@ -212,17 +212,15 @@
         near[way, 1].wait_recv()
         across.append(net.send(part(ring(here.y, -way), 2), here.other_core()))
     yield
+    for copy in across[:3]:
+        copy.wait_recv()
+    yield
     for way in (1, -1):
         onward[way].wait_recv()
         across.append(net.send(part(ring(here.y, 2), far[way]), here.other_core()))
     yield
-    across[0].wait_recv()
-    yield
-    across[1].wait_recv()
-    across[2].wait_recv()
-    yield
-    across[3].wait_recv()
-    across[4].wait_recv()
+    for copy in across[3:]:
+        copy.wait_recv()
 
 
 def token_gather(net, here, part, arrived):
@@ -291,7 +289,8 @@
 class Exchange:
     def __init__(self, moves, sent, landed, base=0):
         self.moves = []
-        for i, (source, target, to, keep) in enumerate(moves, base):
+        for n, (source, target, to, keep) in enumerate(moves):
+            i = base + n
             copy = pltpu.make_async_remote_copy(
                 src_ref=source,
                 dst_ref=target,
@@ -332,18 +331,19 @@
 
 
 PLANE, TOKEN, COLUMN, SMALL = 40, 14, 11, 7
-SINGLE = 7
+SINGLE = 8
 
 
 def layer_kernel(
     scale, tokens, gain, qkv_weight, weight, cosine, sine, q_gain, k_gain, home,
-    tokens_full, gain_full, qkv_full, normed,
+    tokens_full, gain_full, q_weight, kv_weight, normed,
     q_ref, k_ref, v_ref, keys, values, acc, top, heads, out_weight, total, result,
     sent, landed,
 ):
     rows, head_dim = k_ref.shape
     half_rows = rows // 2
     width, depth = tokens.shape[1], tokens_full.shape[1]
+    q_width = GROUP * head_dim
     here = Place()
     factor_log2 = scale * math.log2(math.e)
     greet(
@@ -359,7 +359,7 @@
     stays = jnp.logical_and(here.core == 0, here.z_hi == 0)
     first = Exchange(
         [
-            weight_move(here, qkv_weight, qkv_full),
+            weight_move(here, qkv_weight.at[:, q_width:], kv_weight),
             (tokens.at[:half_rows, :], landing, here.chunk_to(0), stays),
             (tokens.at[half_rows:, :], landing, here.chunk_to(1), None),
             (gain, gain_full.at[:, columns], here.turned(), here.core == here.z_hi),
@@ -375,13 +375,32 @@
         return tokens_full.at[pl.ds(slot, half_rows), pl.ds(start, width)]
 
     first.wait(0)
-    weights = weight_gather(net, here, qkv_full, qkv_weight.shape[0])
-    next(weights)
+    kv_side = weight_gather(net, here, kv_weight, qkv_weight.shape[0])
+    next(kv_side)
     features = token_gather(net, here, token_part, lambda piece: first.wait(1 + piece))
     next(features)
     next(features)
+    turn = Exchange([weight_move(here, qkv_weight.at[:, :q_width], q_weight)], sent, landed, 7)
+    next(kv_side)
     first.wait(3)
-    together(features, weights, small_gather(net, here, gain_full, width))
+    gains = small_gather(net, here, gain_full, width)
+    next(gains)
+    next(kv_side)
+    turn.wait(0)
+    q_side = weight_gather(net, here, q_weight, qkv_weight.shape[0])
+    next(q_side)
+    next(features)
+    next(kv_side)
+    next(features)
+    next(q_side)
+    turn = Exchange([weight_move(here, weight, out_weight)], sent, landed, 4)
+    next(kv_side)
+    next(gains)
+    next(features)
+    next(q_side)
+    together(kv_side, gains)
+    next(q_side)
+    next(features, None)
 
     step, span = 64, 512
     spans = [slice(i, i + span) for i in range(0, depth, span)]
@@ -402,6 +421,8 @@
                 normed.dtype
             )
 
+    next(q_side)
+
     def turned(u, head_gain, where):
         mean_sq = jnp.mean(u * u, axis=-1, keepdims=True)
         u = u * lax.rsqrt(mean_sq + EPSILON) * head_gain
@@ -409,13 +430,12 @@
         return (u * cosine[where, :] + turn * sine[where, :]).astype(jnp.bfloat16)
 
     block = half_rows // 2
-    q_width = GROUP * head_dim
 
     @pl.loop(0, rows // block)
     def _(n):
         where = pl.ds(pl.multiple_of(n * block, block), block)
         both = jnp.dot(
-            normed[where, :], qkv_full[:, q_width:], preferred_element_type=jnp.float32
+            normed[where, :], kv_weight[...], preferred_element_type=jnp.float32
         )
         k_ref[where, :] = turned(both[:, :head_dim], k_gain[...], where)
         v_ref[where, :] = both[:, head_dim:].astype(v_ref.dtype)
@@ -424,12 +444,13 @@
         net, here, (keys, values), rows, lambda half, x, z: (4 * x + z) * rows, (k_ref, v_ref)
     )
     next(arrivals)
+    together(q_side)
 
     @pl.loop(0, rows // block)
     def _(n):
         where = pl.ds(pl.multiple_of(n * block, block), block)
         four = jnp.dot(
-            normed[where, :], qkv_full[:, :q_width], preferred_element_type=jnp.float32
+            normed[where, :], q_weight[...], preferred_element_type=jnp.float32
         )
         for h in range(GROUP):
             cut = slice(h * head_dim, (h + 1) * head_dim)
@@ -438,7 +459,7 @@
     acc[...] = jnp.zeros_like(acc)
     top[...] = jnp.full_like(top, -1e30)
 
-    def unit(which, key_parts, value_parts, allowed=None, among=range(GROUP)):
+    def unit(which, key_parts, value_parts, allowed=None):
         key_block = [ref[...] for ref in key_parts]
         value_block = [ref[...] for ref in value_parts]
         key_block = key_block[0] if len(key_block) == 1 else jnp.concatenate(key_block, axis=0)
@@ -456,10 +477,10 @@
                 preferred_element_type=jnp.float32,
             )
 
-        following = scores(among[0])
-        for h in among:
+        following = scores(0)
+        for h in range(GROUP):
             raw = following
-            if h != among[-1]:
+            if h + 1 < GROUP:
                 following = scores(h + 1)
             if allowed is not None:
                 raw = jnp.where(allowed, raw, -1e30)
@@ -482,19 +503,23 @@
         start = (4 * x + z) * rows + which * half_rows
         return full.at[pl.ds(pl.multiple_of(start, half_rows), half_rows), :]
 
-    def at_once(places, among=range(GROUP)):
-        spots = [(ring(here.x, dx), ring(here.z, dz)) for dx, dz in places]
+    def spots_of(places):
+        return [(ring(here.x, dx), ring(here.z, dz)) for dx, dz in places]
+
+    def their_low(places):
+        spots = spots_of(places)
         unit(
             high,
             [part(keys, x, z, z % 2) for x, z in spots],
             [part(values, x, z, z % 2) for x, z in spots],
-            among=among,
         )
-        for x, z in spots:
+
+    def their_other(places):
+        for x, z in spots_of(places):
             before = (31 + low_chunk(here.x, here.z) - low_chunk(x, z)) // 32
             which = high + before * (low - high)
             theirs = 1 - z % 2 + before * (2 * (z % 2) - 1)
-            unit(which, [part(keys, x, z, theirs)], [part(values, x, z, theirs)], among=among)
+            unit(which, [part(keys, x, z, theirs)], [part(values, x, z, theirs)])
 
     def own(ref, which):
         return ref.at[pl.ds(pl.multiple_of(which * half_rows, half_rows), half_rows), :]
@@ -520,37 +545,42 @@
         for when in steps:
             pl.when(n == when)(lambda: next(arrivals) and None)
         digits = [r % 4 for r in rest]
-        at_once([digits[:2], digits[2:]])
+        their_low([digits[:2], digits[2:]])
+        their_other([digits[:2], digits[2:]])
         return tuple(r // 4 for r in rest)
 
+    turn.wait(0)
+    out_side = weight_gather(net, here, out_weight, weight.shape[0])
+    next(out_side)
     lax.fori_loop(0, len(pairs), stage, tuple(jnp.int32(t) for t in tables))
 
-    turn = Exchange([weight_move(here, weight, out_weight)], sent, landed, 4)
     next(arrivals, None)
-    spread, weights = [], None
-    for h in range(GROUP):
-        at_once([(1, 2), (3, 2)], [h])
-        at_once([(2, 2)], [h])
-        for which in (0, 1):
-            heads[here.column() * GROUP + h, which * half_rows : (which + 1) * half_rows, :] = (
+    rest = [(1, 2), (3, 2), (2, 2)]
+
+    def leave(which):
+        where = pl.ds(pl.multiple_of(which * half_rows, half_rows), half_rows)
+        for h in range(GROUP):
+            heads[here.column() * GROUP + h, where, :] = (
                 acc[which, h, :, :head_dim] / acc[which, h, :, head_dim:]
             ).astype(heads.dtype)
-        spread.append(
-            column_gather(
-                net, here,
-                lambda y, which, h=h: heads.at[
-                    here.column(y) * GROUP + h, rows_of(rows, which), :
-                ],
-            )
-        )
-        next(spread[h])
-        if h == 1:
-            turn.wait(0)
-            weights = weight_gather(net, here, out_weight, weight.shape[0])
-            next(weights)
-    queue = [0, None, 1, 0, None, 2, 1, None, 3, 2, None, 3, 0, None, 1, 2, 3, None]
-    for h in queue:
-        next(weights if h is None else spread[h], None)
+
+        def group(y, piece):
+            first_head, count = (0, GROUP) if piece == 2 else (piece * (GROUP // 2), GROUP // 2)
+            return heads.at[pl.ds(here.column(y) * GROUP + first_head, count), where, :]
+
+        gather = column_gather(net, here, group)
+        next(gather)
+        return gather
+
+    their_other(rest)
+    early = leave(low)
+    their_low(rest)
+    late = leave(high)
+    for side in (
+        early, out_side, early, out_side, late, early, early, out_side, late, out_side,
+        out_side, out_side, early,
+    ):
+        next(side, None)
 
     span = 2 * GROUP * head_dim
 
@@ -564,46 +594,54 @@
             jnp.concatenate(left, axis=1), right, preferred_element_type=jnp.float32
         )
 
-    for i, group in enumerate(((0,), (1, -1))):
-        for h in range(GROUP):
-            next(spread[h])
-        for shift in group:
-
-            @pl.loop(0, rows // block)
-            def _(n):
-                where = pl.ds(pl.multiple_of(n * block, block), block)
-                added = product(ring(here.y, shift), n * block)
-                total[where, :] = added if i == 0 else total[where, :] + added
-
-    for h in range(GROUP):
-        next(spread[h], None)
-    last = []
-    for half in (0, 1):
-        slot = pl.multiple_of(((here.z_hi + half) % 2) * half_rows, half_rows)
-
+    def multiply(which, shifts, opens, closes):
         @pl.loop(0, half_rows // block)
         def _(n):
-            start = slot + n * block
+            start = which * half_rows + n * block
             where = pl.ds(pl.multiple_of(start, block), block)
-            added = product(ring(here.y, 2), start)
-            result[where, :] = (total[where, :] + added).astype(result.dtype)
-
-        stays = jnp.logical_and(here.core == 0, here.z_hi == 0) if half == 0 else None
-        last.append(
-            Exchange(
-                [
-                    (
-                        result.at[pl.ds(slot, half_rows), :],
-                        home.at[half * half_rows : (half + 1) * half_rows, :],
-                        here.chunk_from(half),
-                        stays,
+
+            @pl.loop(0, len(shifts))
+            def _(i):
+                added = product(ring(here.y, shifts[0] + i), start)
+                if opens:
+                    pl.when(i == 0)(lambda: total.__setitem__((where, slice(None)), added))
+                    pl.when(i > 0)(
+                        lambda: total.__setitem__(
+                            (where, slice(None)), total[where, :] + added
+                        )
                     )
-                ],
-                sent, landed, 5 + half,
-            )
+                else:
+                    total[where, :] = total[where, :] + added
+
+            if closes:
+                result[where, :] = total[where, :].astype(result.dtype)
+
+    def go_home(which):
+        half = (which + here.z_hi) % 2
+        return Exchange(
+            [
+                (
+                    result.at[
+                        pl.ds(pl.multiple_of(which * half_rows, half_rows), half_rows), :
+                    ],
+                    home.at[pl.ds(pl.multiple_of(half * half_rows, half_rows), half_rows), :],
+                    here.chunk_from(half),
+                    (1 - here.core) * (1 - here.z_hi) * (1 - half) == 1,
+                )
+            ],
+            sent, landed, 5 + half,
         )
-    for half in (0, 1):
-        last[half].wait(0)
+
+    multiply(low, (-1, 0, 1, 2), True, True)
+    first_home = go_home(low)
+    next(late)
+    multiply(high, (-1, 0, 1), True, False)
+    next(late)
+    next(late, None)
+    multiply(high, (2,), False, True)
+    second_home = go_home(high)
+    first_home.wait(0)
+    second_home.wait(0)
     net.finish()
 
 
@@ -623,7 +661,7 @@
     angles = positions.astype(jnp.float32)[:, None] * freqs[None, :]
     cosine, sine = jnp.cos(angles), jnp.sin(angles)
     bf16, f32 = jnp.bfloat16, jnp.float32
-    copies = SINGLE + 3 * PLANE + TOKEN + SMALL + GROUP * COLUMN
+    copies = SINGLE + 4 * PLANE + TOKEN + SMALL + 2 * COLUMN
     q_width, out_width = GROUP * head_dim, out_weight.shape[1]
     return pl.pallas_call(
         functools.partial(layer_kernel, head_dim ** (-0.5)),
@@ -634,7 +672,8 @@
         scratch_shapes=[
             pltpu.VMEM((rows, n_col * width), bf16),
             pltpu.VMEM((16, n_col * width), bf16),
-            pltpu.VMEM((n_row * qkv_weight.shape[0], qkv_weight.shape[1]), bf16),
+            pltpu.VMEM((n_row * qkv_weight.shape[0], q_width), bf16),
+            pltpu.VMEM((n_row * qkv_weight.shape[0], qkv_weight.shape[1] - q_width), bf16),
             pltpu.VMEM((rows, n_col * width), bf16),
             pltpu.VMEM((rows, q_width), bf16),
             pltpu.VMEM((rows, head_dim), bf16),

time: 165 us -> 175 us (1.061); the launches traced: 164 us -> 172 us
  Pallas kernels: 158 us -> 165 us
    pallas_call x1, Pallas kernels: 158 us -> 165 us  [per_device(): pl.pallas_call(functools.partial(layer_kernel, head_dim ** (-0.5)), out_s...]
where the time goes in v6:
time: 175 us; the launch traced here: 172 us
  Pallas kernels  165 us (94%)
  local copies, waits for them, and re-layouts  3.33 us (2%)
  other arithmetic  3.3 us (2%)
    pallas_call x1, Pallas kernels, per_device(): pl.pallas_call(functools.partial(layer_kernel, head_dim ** (-0.5)), out_s...  165 us

profile of v6, /device:TPU:1, one launch (start us, length us, event | category | flops | bytes accessed | tf_op | source)
XLA Modules:
  0.0 172.1 jit_solution(14972487184060875288)
XLA Ops:
  0.0 0.0 copy-start
  0.1 0.7 copy-done
  0.7 0.6 broadcast_in_dim.6.gain
  1.3 1.4 fusion
  2.8 0.9 pad_maximum_fusion.1.sine
  3.7 0.9 pad_maximum_fusion.cosine
  4.6 165.5 %layer_kernel.1 = bf16[768,512]{1,0:T(8,128)(2,1)} custom-call(bf16[768,512]{1,0:T(8,128)(2,1)} %tokens.1, bf16[16,512]{1,0:T(8,128)(2,1)} %broadcast_in_dim.6.gain, bf16[256,768]{1,0:T(8,128)(2,1)} %qkv_weight.1, bf16[256,512]{1,0:T(8,128)(2,1)} %weight.1, f32[768,128]{1,0:T(8,128)} %pad_maximum_fusion.cosine, f32[768,128]{1,0:T(8,128)} %pad_maximum_fusion.1.sine, ...), custom_call_target="tpu_custom_call" | custom-call | tf_op jit(solution)/shard_map/layer_kernel/pallas_call | solution.py:666
  170.1 2.1 %copy.8 = bf16[768,512]{1,0:T(8,128)(2,1)} copy(bf16[768,512]{1,0:T(8,128)(2,1)} %layer_kernel.1) | data formatting | bytes 1572864
  (3 shorter events, 0.0 us)
Async XLA Ops:
  0.0 0.7 copy-start

commit v7 on v5

--- a/solution.py
+++ b/solution.py
@@ -212,17 +212,15 @@
         near[way, 1].wait_recv()
         across.append(net.send(part(ring(here.y, -way), 2), here.other_core()))
     yield
+    for copy in across[:3]:
+        copy.wait_recv()
+    yield
     for way in (1, -1):
         onward[way].wait_recv()
         across.append(net.send(part(ring(here.y, 2), far[way]), here.other_core()))
     yield
-    across[0].wait_recv()
-    yield
-    across[1].wait_recv()
-    across[2].wait_recv()
-    yield
-    across[3].wait_recv()
-    across[4].wait_recv()
+    for copy in across[3:]:
+        copy.wait_recv()
 
 
 def token_gather(net, here, part, arrived):
@@ -336,8 +334,8 @@
 
 
 def layer_kernel(
-    scale, tokens, gain, qkv_weight, weight, cosine, sine, q_gain, k_gain, home,
-    tokens_full, gain_full, qkv_full, normed,
+    scale, tokens, qkv_weight, weight, gain_row, freqs, q_gain, k_gain, home,
+    gain, cosine, sine, tokens_full, gain_full, qkv_full, normed,
     q_ref, k_ref, v_ref, keys, values, acc, top, heads, out_weight, total, result,
     sent, landed,
 ):
@@ -346,6 +344,7 @@
     width, depth = tokens.shape[1], tokens_full.shape[1]
     here = Place()
     factor_log2 = scale * math.log2(math.e)
+    gain[...] = jnp.broadcast_to(gain_row[...].astype(jnp.float32), gain.shape).astype(gain.dtype)
     greet(
         plane_partners(here)
         + column_partners(here)
@@ -374,6 +373,19 @@
         start = pl.multiple_of(here.column(y) * width, width)
         return tokens_full.at[pl.ds(slot, half_rows), pl.ds(start, width)]
 
+    for which in (0, 1):
+        start = here.chunk(which, here.x, here.z) * half_rows
+
+        @pl.loop(0, half_rows // 64)
+        def _(n):
+            shape = (64, head_dim)
+            lane = lax.broadcasted_iota(jnp.int32, shape, 1)
+            position = start + n * 64 + lax.broadcasted_iota(jnp.int32, shape, 0)
+            angle = position.astype(jnp.float32) * freqs[...]
+            where = pl.ds(pl.multiple_of(which * half_rows + n * 64, 64), 64)
+            cosine[where, :] = jnp.cos(angle)
+            sine[where, :] = jnp.where(lane < head_dim // 2, -1.0, 1.0) * jnp.sin(angle)
+
     first.wait(0)
     weights = weight_gather(net, here, qkv_full, qkv_weight.shape[0])
     next(weights)
@@ -382,6 +394,8 @@
     next(features)
     first.wait(3)
     together(features, weights, small_gather(net, here, gain_full, width))
+
+    turn = Exchange([weight_move(here, weight, out_weight)], sent, landed, 4)
 
     step, span = 64, 512
     spans = [slice(i, i + span) for i in range(0, depth, span)]
@@ -525,9 +539,11 @@
 
     lax.fori_loop(0, len(pairs), stage, tuple(jnp.int32(t) for t in tables))
 
-    turn = Exchange([weight_move(here, weight, out_weight)], sent, landed, 4)
+    turn.wait(0)
     next(arrivals, None)
-    spread, weights = [], None
+    weights = weight_gather(net, here, out_weight, weight.shape[0])
+    next(weights)
+    spread = []
     for h in range(GROUP):
         at_once([(1, 2), (3, 2)], [h])
         at_once([(2, 2)], [h])
@@ -544,11 +560,7 @@
             )
         )
         next(spread[h])
-        if h == 1:
-            turn.wait(0)
-            weights = weight_gather(net, here, out_weight, weight.shape[0])
-            next(weights)
-    queue = [0, None, 1, 0, None, 2, 1, None, 3, 2, None, 3, 0, None, 1, 2, 3, None]
+    queue = [0, None, 1, 0, None, 2, 1, None, 3, 2, None, 3, None, 0, 1, None, 2, 3]
     for h in queue:
         next(weights if h is None else spread[h], None)
 
@@ -564,16 +576,22 @@
             jnp.concatenate(left, axis=1), right, preferred_element_type=jnp.float32
         )
 
-    for i, group in enumerate(((0,), (1, -1))):
-        for h in range(GROUP):
-            next(spread[h])
-        for shift in group:
-
-            @pl.loop(0, rows // block)
-            def _(n):
-                where = pl.ds(pl.multiple_of(n * block, block), block)
-                added = product(ring(here.y, shift), n * block)
-                total[where, :] = added if i == 0 else total[where, :] + added
+    for h in (0, 1):
+        next(spread[h])
+
+    @pl.loop(0, rows // block)
+    def _(n):
+        where = pl.ds(pl.multiple_of(n * block, block), block)
+        total[where, :] = product(here.y, n * block)
+
+    for h in (2, 3):
+        next(spread[h])
+    for shift in (1, -1):
+
+        @pl.loop(0, rows // block)
+        def _(n):
+            where = pl.ds(pl.multiple_of(n * block, block), block)
+            total[where, :] = total[where, :] + product(ring(here.y, shift), n * block)
 
     for h in range(GROUP):
         next(spread[h], None)
@@ -612,26 +630,23 @@
     rows, width = tokens.shape
     half = rows // 2
     head_dim = q_gain.shape[0]
-    here = Place()
-    chunks = [here.chunk(which, here.x, here.z) for which in (0, 1)]
-    within = jnp.arange(half, dtype=jnp.int32)
-    positions = jnp.concatenate([chunk * half + within for chunk in chunks])
     freqs = jnp.power(
         jnp.float32(ROPE_BASE),
         -jnp.arange(head_dim // 2, dtype=jnp.float32) * 2.0 / head_dim,
     )
-    angles = positions.astype(jnp.float32)[:, None] * freqs[None, :]
-    cosine, sine = jnp.cos(angles), jnp.sin(angles)
     bf16, f32 = jnp.bfloat16, jnp.float32
     copies = SINGLE + 3 * PLANE + TOKEN + SMALL + GROUP * COLUMN
     q_width, out_width = GROUP * head_dim, out_weight.shape[1]
     return pl.pallas_call(
         functools.partial(layer_kernel, head_dim ** (-0.5)),
         out_shape=jax.ShapeDtypeStruct((rows, out_width), bf16),
-        in_specs=[pl.BlockSpec(memory_space=pl.ANY)] * 4
+        in_specs=[pl.BlockSpec(memory_space=pl.ANY)] * 3
         + [pl.BlockSpec(memory_space=pltpu.VMEM)] * 4,
         out_specs=pl.BlockSpec(memory_space=pl.ANY),
         scratch_shapes=[
+            pltpu.VMEM((16, width), bf16),
+            pltpu.VMEM((rows, head_dim), f32),
+            pltpu.VMEM((rows, head_dim), f32),
             pltpu.VMEM((rows, n_col * width), bf16),
             pltpu.VMEM((16, n_col * width), bf16),
             pltpu.VMEM((n_row * qkv_weight.shape[0], qkv_weight.shape[1]), bf16),
@@ -651,16 +666,15 @@
             pltpu.SemaphoreType.DMA((copies,)),
         ],
         compiler_params=pltpu.CompilerParams(
-            collective_id=1, has_side_effects=True, vmem_limit_bytes=60 * 1024 * 1024
+            collective_id=1, has_side_effects=True, vmem_limit_bytes=54 * 1024 * 1024
         ),
         name="layer_kernel",
     )(
         tokens,
-        jnp.broadcast_to(norm_gain[None, :], (16, width)),
         qkv_weight,
         out_weight,
-        jnp.concatenate([cosine, cosine], axis=1),
-        jnp.concatenate([-sine, sine], axis=1),
+        norm_gain[None, :],
+        jnp.concatenate([freqs, freqs])[None, :],
         q_gain[None, :],
         k_gain[None, :],
     )

time: 165 us -> 160 us (0.970)
  other arithmetic: 3.3 us -> 0.57 us
  Pallas kernels: 158 us -> 156 us
    concatenate x2 -> x0, other arithmetic: 1.83 us -> none  [the longest x1 0.92 us: per_device(): jnp.concatenate([cosine, cosine], axis=1)]
where the time goes in v7:
time: 160 us
  Pallas kernels  156 us (98%)
  local copies, waits for them, and re-layouts  2.76 us (2%)
    pallas_call x1, Pallas kernels, per_device(): pl.pallas_call(functools.partial(layer_kernel, head_dim ** (-0.5)), out_s...  156 us

profile of v7, /device:TPU:1, one launch (start us, length us, event | category | flops | bytes accessed | tf_op | source)
XLA Modules:
  0.0 159.7 jit_solution(3105614303882572155)
XLA Ops:
  0.0 0.0 copy-start
  0.0 0.6 maximum_bitcast_fusion.freqs
  0.6 0.1 copy-done
  0.7 0.6 broadcast_in_dim.12.gain_row
  1.3 156.3 %layer_kernel.1 = bf16[768,512]{1,0:T(8,128)(2,1)} custom-call(bf16[768,512]{1,0:T(8,128)(2,1)} %tokens.1, bf16[256,768]{1,0:T(8,128)(2,1)} %qkv_weight.1, bf16[256,512]{1,0:T(8,128)(2,1)} %weight.1, bf16[1,512]{1,0:T(2,128)(2,1)} %broadcast_in_dim.12.gain_row, f32[1,128]{1,0:T(1,128)} %maximum_bitcast_fusion.freqs, f32[1,128]{1,0:T(1,128)} %bitcast.4, ...), custom_call_target="tpu_custom_call" | custom-call | tf_op jit(solution)/shard_map/layer_kernel/pallas_call | solution.py:640
  157.6 2.1 %copy.8 = bf16[768,512]{1,0:T(8,128)(2,1)} copy(bf16[768,512]{1,0:T(8,128)(2,1)} %layer_kernel.1) | data formatting | bytes 1572864
  (1 shorter events, 0.0 us)
Async XLA Ops:
  0.0 0.7 copy-start

commit v8 on v7

--- a/solution.py
+++ b/solution.py
@@ -479,7 +479,7 @@
                 raw = jnp.where(allowed, raw, -1e30)
             before = top[which, h]
             now = jnp.maximum(before, jnp.max(raw, axis=-1, keepdims=True))
-            shift = now[:, :1] * factor_log2
+            shift = jnp.concatenate([now * factor_log2] * (raw.shape[1] // head_dim), axis=1)
             weights = jnp.exp2(raw * factor_log2 - shift).astype(jnp.bfloat16)
             fade = jnp.exp2((before - now) * factor_log2)
             added = jnp.dot(weights, wide, preferred_element_type=jnp.float32)

time: 160 us -> 157 us (0.981)
  Pallas kernels: 156 us -> 153 us
    pallas_call x1, Pallas kernels: 156 us -> 153 us  [per_device(): pl.pallas_call(functools.partial(layer_kernel, head_dim ** (-0.5)), out_s...]
where the time goes in v8:
time: 157 us
  Pallas kernels  153 us (97%)
  local copies, waits for them, and re-layouts  2.76 us (2%)
    pallas_call x1, Pallas kernels, per_device(): pl.pallas_call(functools.partial(layer_kernel, head_dim ** (-0.5)), out_s...  153 us

profile of v8, /device:TPU:1, one launch (start us, length us, event | category | flops | bytes accessed | tf_op | source)
XLA Modules:
  0.0 156.6 jit_solution(16096548486573140570)
XLA Ops:
  0.0 0.0 copy-start
  0.0 0.6 maximum_bitcast_fusion.freqs
  0.6 0.1 copy-done
  0.7 0.6 broadcast_in_dim.12.gain_row
  1.3 153.3 %layer_kernel.1 = bf16[768,512]{1,0:T(8,128)(2,1)} custom-call(bf16[768,512]{1,0:T(8,128)(2,1)} %tokens.1, bf16[256,768]{1,0:T(8,128)(2,1)} %qkv_weight.1, bf16[256,512]{1,0:T(8,128)(2,1)} %weight.1, bf16[1,512]{1,0:T(2,128)(2,1)} %broadcast_in_dim.12.gain_row, f32[1,128]{1,0:T(1,128)} %maximum_bitcast_fusion.freqs, f32[1,128]{1,0:T(1,128)} %bitcast.4, ...), custom_call_target="tpu_custom_call" | custom-call | tf_op jit(solution)/shard_map/layer_kernel/pallas_call | solution.py:640
  154.6 2.1 %copy.8 = bf16[768,512]{1,0:T(8,128)(2,1)} copy(bf16[768,512]{1,0:T(8,128)(2,1)} %layer_kernel.1) | data formatting | bytes 1572864
  (1 shorter events, 0.0 us)
Async XLA Ops:
  0.0 0.7 copy-start

commit v9 on v8

--- a/solution.py
+++ b/solution.py
@@ -666,7 +666,7 @@
             pltpu.SemaphoreType.DMA((copies,)),
         ],
         compiler_params=pltpu.CompilerParams(
-            collective_id=1, has_side_effects=True, vmem_limit_bytes=54 * 1024 * 1024
+            collective_id=1, has_side_effects=True, vmem_limit_bytes=52 * 1024 * 1024
         ),
         name="layer_kernel",
     )(

time: 157 us -> 156 us (level)
  Pallas kernels: 153 us -> 151 us
    pallas_call x1, Pallas kernels: 153 us -> 151 us  [per_device(): pl.pallas_call(functools.partial(layer_kernel, head_dim ** (-0.5)), out_s...]
    unnamed x3 -> x11, local copies, waits for them, and re-layouts: 2.18 us -> 4.09 us
where the time goes in v9:
time: 156 us; the launch traced here: 155 us
  Pallas kernels  151 us (97%)
  local copies, waits for them, and re-layouts  4.1 us (3%)
    pallas_call x1, Pallas kernels, per_device(): pl.pallas_call(functools.partial(layer_kernel, head_dim ** (-0.5)), out_s...  151 us
    unnamed x11, local copies, waits for them, and re-layouts  4.09 us

profile of v9, /device:TPU:1, one launch (start us, length us, event | category | flops | bytes accessed | tf_op | source)
XLA Modules:
  0.0 155.4 jit_solution(7077707704610928958)
XLA Ops:
  0.0 0.0 copy-start.4
  0.0 0.1 maximum_bitcast_fusion.freqs
  0.1 0.6 copy-done.4
  0.7 0.0 copy-start.2
  0.7 0.0 copy-start.3
  0.7 0.6 copy-done.2
  1.4 0.0 copy-done.3
  1.4 0.0 copy-start
  1.4 1.0 copy-done
  2.4 0.0 copy-start.1
  2.4 0.9 copy-done.1
  3.3 151.2 %layer_kernel.1 = bf16[768,512]{1,0:T(8,128)(2,1)S(1)} custom-call(bf16[768,512]{1,0:T(8,128)(2,1)} %tokens.1, bf16[256,768]{1,0:T(8,128)(2,1)S(1)} %copy-done, bf16[256,512]{1,0:T(8,128)(2,1)S(1)} %copy-done.1, bf16[1,512]{1,0:T(2,128)(2,1)S(1)} %broadcast_in_dim.12.gain_row, f32[1,128]{1,0:T(1,128)S(1)} %maximum_bitcast_fusion.freqs, ...), custom_call_target="tpu_custom_call" | custom-call | tf_op jit(solution)/shard_map/layer_kernel/pallas_call | solution.py:640
  154.5 0.9 copy.8
  (2 shorter events, 0.0 us)
Async XLA Ops:
  0.0 0.7 copy-start.4
  0.7 0.7 copy-start.2
  0.7 0.7 copy-start.3
  1.4 1.0 copy-start
  2.4 0.9 copy-start.1
